TPU v7x, 128 devices: a whole 4x4x4 slice. The times are simulated.
128 devices in a mesh: seq: 8 (over z, core), tp: 16 (over x, y).
Axes of the slice: x: 4, y: 4, z: 4, core: 2. Of those that a mesh axis runs over, the one named last changes fastest.
Arguments:
- sequence_in: bfloat16 [1536, 4096], P('tp', 'seq')
- conv_weight: bfloat16 [3, 1536, 3, 1536], P(None, 'tp')
- norm_gain: float32 [3, 1536], P(None, 'tp'), may hold values from 0.1 to 1.9
- tissue_scale: float32 [367, 1536], replicated, may hold values from 0.3 to 3
- donor_offset: int32 [2048], P('seq'), may hold values from 0 to 511
- acceptor_owner: int32 [2048, 1], P('seq'), may hold values from 0 to 7; in each aligned block of 256 rows (0 to 255, 256 to 511, ...) at most 128 rows name the same one
- acceptor_offset: int32 [2048], P('seq'), may hold values from 0 to 511
- tissue: int32 [2048], P('seq'), may hold values from 0 to 366
- tower_grad: float32 [1536, 4096], P('tp', 'seq'), may hold values from -6 to 6
- score_grad: float32 [2048], P('seq'), may hold values from -24 to 24
Outputs:
- scores: float32 [2048], P('seq')
- input_grad: float32 [1536, 4096], P('tp', 'seq')
- weight_grad: float32 [3, 1536, 3, 1536], P(None, 'tp')
- gain_grad: float32 [3, 1536], P(None, 'tp')
Inputs may be any that keep to these rules, and one draw needn't show every extreme that they name: `acceptor_owner`: among the 256 junctions of one index of seq, at most 128 have their acceptor on one index of seq.
All inputs are finite; a program needn't handle non-finite values.
Results may differ from a plain program's by a relative error of at most 0.025.
Values may be sent and summed in bfloat16 or wider, within the bound.
A program may use at most 128 MiB of HBM per device.

v0:
```python
import math

import jax
import jax.numpy as jnp
from jax import lax
from jax.sharding import PartitionSpec as P

CHANNELS = 1536
LAYERS = 3
CAP = 128


EPSILON = 1e-06


def with_halo(x, sides, width):
    for axis, dim in sides:
        count, length = (lax.axis_size(axis), x.shape[dim])
        up = [(i, (i + 1) % count) for i in range(count - 1)]
        down = [(j, i) for i, j in up]
        last = lax.slice_in_dim(x, length - width, length, axis=dim)
        initial = lax.slice_in_dim(x, 0, width, axis=dim)
        before = lax.ppermute(last, axis, up)
        after = lax.ppermute(initial, axis, down)
        x = jnp.concatenate([before, x, after], axis=dim)
    return x


def gelu_fn(value):
    return jax.nn.gelu(value, approximate=True)


def widen(block, width):
    return with_halo(block, (("seq", 1),), width)


def forward_taps(weights, padded, reach, length):
    total = jnp.zeros((weights.shape[0], length), jnp.float32)
    for tap in range(3):
        total = total + jnp.dot(
            weights[:, tap, :],
            padded[:, tap * reach : tap * reach + length],
            preferred_element_type=jnp.float32,
        )
    return total


def backward_taps(weights, grad_pad, reach, length):
    total = jnp.zeros((weights.shape[2], length), jnp.float32)
    for tap in range(3):
        total = total + lax.dot_general(
            weights[:, tap, :],
            grad_pad[:, (2 - tap) * reach : (2 - tap) * reach + length],
            (((0,), (0,)), ((), ())),
            preferred_element_type=jnp.float32,
        )
    return total


def weight_taps(padded, grad_bf, reach, length):
    blocks = []
    for tap in range(3):
        blocks.append(
            lax.dot_general(
                grad_bf,
                padded[:, tap * reach : tap * reach + length],
                (((1,), (1,)), ((), ())),
                preferred_element_type=jnp.float32,
            )
        )
    return jnp.stack(blocks, axis=1)


def local(
    sequence_in,
    conv_weight,
    norm_gain,
    tissue_scale,
    donor_offset,
    acceptor_owner,
    acceptor_offset,
    tissue,
    tower_grad,
    score_grad,
):
    local_ch = sequence_in.shape[0]
    length = sequence_in.shape[1]
    seq_count = lax.axis_size("seq")
    state = sequence_in
    stored = []
    for layer in range(LAYERS):
        reach = 2 ** (layer + 3)
        stream = state.astype(jnp.float32)
        power = lax.psum(jnp.sum(stream * stream, axis=0), "tp") / CHANNELS
        inverse = 1.0 / jnp.sqrt(power + EPSILON)
        pre_act = stream * inverse[None, :] * norm_gain[layer][:, None]
        hidden = gelu_fn(pre_act).astype(jnp.bfloat16)
        padded = widen(hidden, reach)
        weights = conv_weight[layer]
        gathered = padded

        def fold_inputs(total, piece, start, weights=weights, reach=reach):
            return forward_taps(weights, piece, reach, length)

        mixed = fold_inputs(
            jnp.zeros((local_ch, length), jnp.float32),
            lax.all_gather(padded, "tp", axis=0, tiled=True),
            jnp.int32(0),
        )
        stored.append((state, inverse, pre_act, gathered))
        state = (stream + mixed).astype(jnp.bfloat16)
    owner = acceptor_owner[:, 0]
    member = (owner[:, None] == jnp.arange(seq_count, dtype=jnp.int32)[None, :]).astype(jnp.int32)
    slot = jnp.sum(jnp.cumsum(member, axis=0) * member, axis=1) - 1
    requests = jnp.zeros((seq_count, CAP), jnp.int32).at[owner, slot].set(acceptor_offset)
    rows_view = state.T
    offsets = lax.all_to_all(requests, "seq", split_axis=0, concat_axis=0, tiled=True)
    picked = rows_view[offsets]
    returned = lax.all_to_all(picked, "seq", split_axis=0, concat_axis=0, tiled=True)
    accept_cols = returned[owner, slot].astype(jnp.float32)
    donor_cols = rows_view[donor_offset].astype(jnp.float32)
    chan_start = lax.axis_index("tp") * local_ch
    local_table = lax.dynamic_slice_in_dim(tissue_scale, chan_start, local_ch, 1)
    tissue_hit = (
        tissue[:, None] == jnp.arange(tissue_scale.shape[0], dtype=jnp.int32)[None, :]
    ).astype(jnp.float32)
    tissue_rows = jnp.dot(tissue_hit, local_table, precision=lax.Precision.HIGHEST)
    root = math.sqrt(CHANNELS)
    partial_scores = jnp.sum(donor_cols * accept_cols * tissue_rows, axis=1) / root
    scores = lax.psum(partial_scores, "tp")
    weight_j = score_grad / root
    donor_back = weight_j[:, None] * accept_cols * tissue_rows
    accept_back = weight_j[:, None] * donor_cols * tissue_rows
    outgoing = jnp.zeros((seq_count, CAP, local_ch), jnp.float32).at[owner, slot].set(accept_back)
    incoming = lax.all_to_all(
        outgoing.astype(jnp.bfloat16), "seq", split_axis=0, concat_axis=0, tiled=True
    ).astype(outgoing.dtype)
    upstream = tower_grad.at[:, donor_offset].add(donor_back.T)
    upstream = upstream.at[:, offsets.reshape(-1)].add(incoming.reshape(-1, local_ch).T)
    weight_list = [None] * LAYERS
    gain_list = [None] * LAYERS
    for layer in reversed(range(LAYERS)):
        reach = 2 ** (layer + 3)
        old_state, inverse, pre_act, gathered = stored[layer]
        stream = old_state.astype(jnp.float32)
        grad_bf = upstream.astype(jnp.bfloat16)
        grad_pad = widen(grad_bf, reach)
        weights = conv_weight[layer]

        def term_rows(start, count, weights=weights, grad_pad=grad_pad, reach=reach):
            return backward_taps(weights, grad_pad, reach, length)

        back_hidden = lax.psum_scatter(
            term_rows(jnp.int32(0), local_ch * lax.axis_size("tp")).astype(jnp.bfloat16),
            "tp",
            scatter_dimension=0,
            tiled=True,
        ).astype(jnp.float32)

        def fold_weights(total, piece, start, grad_bf=grad_bf, reach=reach):
            return weight_taps(piece, grad_bf, reach, length)

        weight_term = fold_weights(
            jnp.zeros((local_ch, 3, CHANNELS), jnp.float32),
            lax.all_gather(gathered, "tp", axis=0, tiled=True),
            jnp.int32(0),
        )
        weight_list[layer] = lax.psum(weight_term.astype(jnp.bfloat16), "seq").astype(jnp.float32)
        _, gelu_back = jax.vjp(gelu_fn, pre_act)
        back_pre = gelu_back(back_hidden)[0]
        gain_list[layer] = jnp.sum(back_pre * stream * inverse[None, :], axis=1)
        back_norm = back_pre * norm_gain[layer][:, None]
        inner = lax.psum(jnp.sum(back_norm * stream, axis=0), "tp")
        upstream = (
            upstream
            + inverse[None, :] * back_norm
            - stream * (inverse**3)[None, :] * inner[None, :] / CHANNELS
        )
    gain_grad = lax.psum(jnp.stack(gain_list), "seq")
    return (scores, upstream, jnp.stack(weight_list), gain_grad)


def solution(mesh):
    return jax.shard_map(
        local,
        mesh=mesh,
        in_specs=(
            P("tp", "seq"),
            P(None, "tp", None, None),
            P(None, "tp"),
            P(),
            P("seq"),
            P("seq", None),
            P("seq"),
            P("seq"),
            P("tp", "seq"),
            P("seq"),
        ),
        out_specs=(P("seq"), P("tp", "seq"), P(None, "tp", None, None), P(None, "tp")),
        check_vma=False,
    )
```

profile of v0, /device:TPU:1, one launch (start us, length us, event | category | flops | bytes accessed | tf_op | source)
XLA Modules:
  0.0 806.4 jit_solution(14602728577334916671)
XLA Ops:
  9.6 34.2 %psum.77 = f32[512]{0:T(512)S(1)} all-reduce(f32[512]{0:T(512)S(1)} %fusion.133), channel_id=1, replica_groups=mesh['seq'=8,'tp'=16] {'tp'}, use_global_device_ids=true, to_apply=%region_1.0 | all-reduce | flops 512 | bytes 4096 | tf_op jit(solution)/shard_map/psum | solution.py:94
  45.6 11.3 %collective-permute-start = (bf16[96,8]{1,0:T(8,128)(2,1)S(1)}, bf16[96,8]{1,0:T(8,128)(2,1)S(1)}, u32[]{:S(2)}, u32[]{:S(2)}) collective-permute-start(bf16[96,8]{1,0:T(8,128)(2,1)S(1)} %get-tuple-element.37), channel_id=1, source_target_pairs={{0,16},{16,32},{32,48},{48,64},{64,80},{80,96},{96,112},{1,17},{17... | collective-permute-start | bytes 4616 | tf_op jit(solution)/shard_map/ppermute | solution.py:23
  66.1 36.3 %all-gather.4.cloned.1.call-done = bf16[1536,528]{1,0:T(8,128)(2,1)} async-done(((bf16[96,528]{1,0:T(8,128)(2,1)}), bf16[1536,528]{1,0:T(8,128)(2,1)}) %all-gather.4.cloned.1.call-update) | async-done | bytes 1622032 | tf_op jit(solution)/shard_map/all_gather | solution.py:107
  107.4 30.9 %psum.78 = f32[512]{0:T(512)S(1)} all-reduce(f32[512]{0:T(512)S(1)} %get-tuple-element.50), channel_id=1, replica_groups=mesh['seq'=8,'tp'=16] {'tp'}, use_global_device_ids=true, to_apply=%region_3.0 | all-reduce | flops 512 | bytes 4096 | tf_op jit(solution)/shard_map/psum | solution.py:94
  139.2 12.4 %collective-permute-start.2 = (bf16[96,16]{1,0:T(8,128)(2,1)S(1)}, bf16[96,16]{1,0:T(8,128)(2,1)S(1)}, u32[]{:S(2)}, u32[]{:S(2)}) collective-permute-start(bf16[96,16]{1,0:T(8,128)(2,1)S(1)} %get-tuple-element.35), channel_id=1, source_target_pairs={{0,16},{16,32},{32,48},{48,64},{64,80},{80,96},{96,112},{1,17},{17... | collective-permute-start | bytes 9224 | tf_op jit(solution)/shard_map/ppermute | solution.py:23
  157.6 38.8 %all-gather.6.cloned.1.call-done = bf16[1536,544]{1,0:T(8,128)(2,1)} async-done(((bf16[96,544]{1,0:T(8,128)(2,1)}), bf16[1536,544]{1,0:T(8,128)(2,1)}) %all-gather.6.cloned.1.call-update) | async-done | bytes 1671184 | tf_op jit(solution)/shard_map/all_gather | solution.py:107
  199.8 31.0 %psum.79 = f32[512]{0:T(512)S(1)} all-reduce(f32[512]{0:T(512)S(1)} %get-tuple-element.52), channel_id=1, replica_groups=mesh['seq'=8,'tp'=16] {'tp'}, use_global_device_ids=true, to_apply=%region_5.0 | all-reduce | flops 512 | bytes 4096 | tf_op jit(solution)/shard_map/psum | solution.py:94
  232.3 12.4 %collective-permute-start.4 = (bf16[96,32]{1,0:T(8,128)(2,1)S(1)}, bf16[96,32]{1,0:T(8,128)(2,1)S(1)}, u32[]{:S(2)}, u32[]{:S(2)}) collective-permute-start(bf16[96,32]{1,0:T(8,128)(2,1)S(1)} %get-tuple-element.33), channel_id=1, source_target_pairs={{0,16},{16,32},{32,48},{48,64},{64,80},{80,96},{96,112},{1,17},{17... | collective-permute-start | bytes 18440 | tf_op jit(solution)/shard_map/ppermute | solution.py:23
  252.3 38.6 %scatter_fusion = s32[8,128]{1,0:T(8,128)} fusion(s32[8,128]{1,0:T(8,128)} %broadcast.150, s32[256]{0:T(256)S(1)} %bitcast.150, s32[256]{0:T(256)} %param.16), kind=kCustom, calls=%fused_computation.3 | custom fusion | bytes 5120 | tf_op jit(solution)/shard_map/scatter | solution.py:115
  313.9 4.9 all-to-all-done.1
  322.7 16.8 %scatter_fusion.2 = f32[8,128,96]{2,1,0:T(8,128)S(1)} fusion(f32[8,128,96]{2,1,0:T(8,128)S(1)} %broadcast_in_dim.5, s32[256]{0:T(256)S(1)} %bitcast.151, f32[256,96]{1,0:T(8,128)} %copy.100), kind=kCustom, calls=%fused_computation.5 | custom fusion | bytes 296960 | tf_op jit(solution)/shard_map/scatter | solution.py:134
  340.2 4.9 all-to-all-start.2
  352.1 7.4 scatter_fusion.3
  371.2 67.7 %reduce-scatter.4.cloned.1.call-done = bf16[96,512]{1,0:T(8,128)(2,1)} async-done(((bf16[1536,512]{1,0:T(8,128)(2,1)}), bf16[96,512]{1,0:T(8,128)(2,1)}) %reduce-scatter.4.cloned.1.call-update) | async-done | bytes 98320 | tf_op jit(solution)/shard_map/reduce_scatter | solution.py:153
  440.2 30.9 %psum.81 = f32[512]{0:T(512)S(1)} all-reduce(f32[512]{0:T(512)S(1)} %get-tuple-element.7), channel_id=1, replica_groups=mesh['seq'=8,'tp'=16] {'tp'}, use_global_device_ids=true, to_apply=%region_17.18 | all-reduce | flops 512 | bytes 4096 | tf_op jit(solution)/shard_map/psum | solution.py:173
  473.0 12.7 %collective-permute-start.9 = (bf16[96,16]{1,0:T(8,128)(2,1)S(1)}, bf16[96,16]{1,0:T(8,128)(2,1)S(1)}, u32[]{:S(2)}, u32[]{:S(2)}) collective-permute-start(bf16[96,16]{1,0:T(8,128)(2,1)S(1)} %get-tuple-element.32), channel_id=1, source_target_pairs={{0,16},{16,32},{32,48},{48,64},{64,80},{80,96},{96,112},{1,17},{17... | collective-permute-start | bytes 9224 | tf_op jit(solution)/shard_map/ppermute | solution.py:23
  502.7 60.1 %reduce-scatter.6.cloned.1.call-done = bf16[96,512]{1,0:T(8,128)(2,1)} async-done(((bf16[1536,512]{1,0:T(8,128)(2,1)}), bf16[96,512]{1,0:T(8,128)(2,1)}) %reduce-scatter.6.cloned.1.call-update) | async-done | bytes 98320 | tf_op jit(solution)/shard_map/reduce_scatter | solution.py:153
  564.0 31.1 %psum.82 = f32[512]{0:T(512)S(1)} all-reduce(f32[512]{0:T(512)S(1)} %get-tuple-element.5), channel_id=1, replica_groups=mesh['seq'=8,'tp'=16] {'tp'}, use_global_device_ids=true, to_apply=%region_20.21 | all-reduce | flops 512 | bytes 4096 | tf_op jit(solution)/shard_map/psum | solution.py:173
  601.3 12.6 %collective-permute-start.11 = (bf16[96,8]{1,0:T(8,128)(2,1)S(1)}, bf16[96,8]{1,0:T(8,128)(2,1)S(1)}, u32[]{:S(2)}, u32[]{:S(2)}) collective-permute-start(bf16[96,8]{1,0:T(8,128)(2,1)S(1)} %get-tuple-element.30), channel_id=1, source_target_pairs={{0,16},{16,32},{32,48},{48,64},{64,80},{80,96},{96,112},{1,17},{17... | collective-permute-start | bytes 4616 | tf_op jit(solution)/shard_map/ppermute | solution.py:23
  622.0 50.6 %all-reduce.4.cloned.1.call-done = (bf16[1,96,3,1536]{3,1,2,0:T(8,128)(2,1)}, bf16[1,96,3,1536]{3,1,2,0:T(8,128)(2,1)}, bf16[1,96,3,1536]{3,1,2,0:T(8,128)(2,1)}) async-done(((bf16[1,96,3,1536]{3,1,2,0:T(8,128)(2,1)}, bf16[1,96,3,1536]{3,1,2,0:T(8,128)(2,1)}, bf16[1,96,3,1536]{3,1,2,0:T(8,128)(2,1)}), (bf16[1,96,3,1536]{3,1,2,0:T(8,128)(2,1)}, bf16[1,96,3,1536]{3,1,2,0:T(8,128)(2,1)}, ...) | async-done | bytes 2654224 | tf_op jit(solution)/shard_map/psum | solution.py:168
  672.7 4.5 maximum_convert_fusion
  677.2 73.0 %reduce-scatter.8.cloned.1.call-done = bf16[96,512]{1,0:T(8,128)(2,1)} async-done(((bf16[1536,512]{1,0:T(8,128)(2,1)}), bf16[96,512]{1,0:T(8,128)(2,1)}) %reduce-scatter.8.cloned.1.call-update) | async-done | bytes 98320 | tf_op jit(solution)/shard_map/reduce_scatter | solution.py:153
  751.5 14.8 %psum.87 = f32[3,96]{1,0:T(4,128)} all-reduce(f32[3,96]{1,0:T(4,128)S(1)} %pad_maximum_fusion.15), channel_id=1, replica_groups=mesh['seq'=8,'tp'=16] {'seq'}, use_global_device_ids=true, to_apply=%region_30.31 | all-reduce | flops 288 | bytes 2304 | tf_op jit(solution)/shard_map/psum | solution.py:179
  766.3 31.4 %all-reduce = (f32[256]{0:T(256)}, f32[512]{0:T(512)S(1)}) all-reduce(f32[256]{0:T(256)S(1)} %broadcast_multiply_fusion.1, f32[512]{0:T(512)S(1)} %get-tuple-element.9), channel_id=1, replica_groups=mesh['seq'=8,'tp'=16] {'tp'}, use_global_device_ids=true, to_apply=%region_11.12 | all-reduce | flops 768 | bytes 6144 | tf_op jit(solution)/shard_map/psum | solution.py:130
  (192 shorter events, 122.0 us)
Async XLA Ops:
  7.2 313.6 %copy-start = (f32[367,1536]{1,0:T(8,128)S(1)}, f32[367,1536]{1,0:T(8,128)}, u32[]{:S(2)}) copy-start(f32[367,1536]{1,0:T(8,128)} %param.13) | copy-start | bytes 6764548
  7.2 95.2 %all-gather.4.cloned.1.call-start = ((), (), s32[]{:S(2)}) async-start(), calls=%async_computation.6 | async-start | bytes 2088960 | tf_op jit(solution)/shard_map/all_gather | solution.py:107
  45.6 13.3 %collective-permute-start = (bf16[96,8]{1,0:T(8,128)(2,1)S(1)}, bf16[96,8]{1,0:T(8,128)(2,1)S(1)}, u32[]{:S(2)}, u32[]{:S(2)}) collective-permute-start(bf16[96,8]{1,0:T(8,128)(2,1)S(1)} %get-tuple-element.37), channel_id=1, source_target_pairs={{0,16},{16,32},{32,48},{48,64},{64,80},{80,96},{96,112},{1,17},{17... | collective-permute-start | bytes 4616 | tf_op jit(solution)/shard_map/ppermute | solution.py:23
  56.9 5.1 collective-permute-start.1
  62.8 133.5 %all-gather.6.cloned.1.call-start = ((), (), s32[]{:S(2)}) async-start(), calls=%async_computation.7 | async-start | bytes 2088960 | tf_op jit(solution)/shard_map/all_gather | solution.py:107
  66.1 133.3 %copy-start.1 = (bf16[96,3,1536]{2,0,1:T(8,128)(2,1)}, bf16[96,3,1536]{2,0,1:T(8,128)(2,1)S(1)}, u32[]{:S(2)}) copy-start(bf16[96,3,1536]{2,0,1:T(8,128)(2,1)S(1)} %get-tuple-element.23) | copy-start | bytes 2654212
  139.2 14.4 %collective-permute-start.2 = (bf16[96,16]{1,0:T(8,128)(2,1)S(1)}, bf16[96,16]{1,0:T(8,128)(2,1)S(1)}, u32[]{:S(2)}, u32[]{:S(2)}) collective-permute-start(bf16[96,16]{1,0:T(8,128)(2,1)S(1)} %get-tuple-element.35), channel_id=1, source_target_pairs={{0,16},{16,32},{32,48},{48,64},{64,80},{80,96},{96,112},{1,17},{17... | collective-permute-start | bytes 9224 | tf_op jit(solution)/shard_map/ppermute | solution.py:23
  151.6 5.1 collective-permute-start.3
  157.5 142.2 %all-gather.8.cloned.1.call-start = ((), (), s32[]{:S(2)}) async-start(), calls=%async_computation.8 | async-start | bytes 2088960 | tf_op jit(solution)/shard_map/all_gather | solution.py:107
  232.3 14.4 %collective-permute-start.4 = (bf16[96,32]{1,0:T(8,128)(2,1)S(1)}, bf16[96,32]{1,0:T(8,128)(2,1)S(1)}, u32[]{:S(2)}, u32[]{:S(2)}) collective-permute-start(bf16[96,32]{1,0:T(8,128)(2,1)S(1)} %get-tuple-element.33), channel_id=1, source_target_pairs={{0,16},{16,32},{32,48},{48,64},{64,80},{80,96},{96,112},{1,17},{17... | collective-permute-start | bytes 18440 | tf_op jit(solution)/shard_map/ppermute | solution.py:23
  244.7 5.1 collective-permute-start.5
  290.9 8.8 %all-to-all-start = ((s32[8,1,128]{2,1,0:T(1,128)}), s32[8,1,128]{2,1,0:T(1,128)S(1)}, u32[]{:S(2)}, u32[]{:S(2)}) async-start(s32[8,1,128]{2,1,0:T(1,128)} %bitcast.27), calls=%async_computation | async-start | bytes 8192 | tf_op jit(solution)/shard_map/all_to_all | solution.py:117
  309.0 9.9 %all-to-all-start.1 = ((bf16[8,128,96]{1,2,0:T(8,128)(2,1)}), bf16[8,128,96]{1,2,0:T(8,128)(2,1)S(1)}, u32[]{:S(2)}, u32[]{:S(2)}) async-start(bf16[8,128,96]{1,2,0:T(8,128)(2,1)} %copy.95), calls=%async_computation.1 | async-start | bytes 393216 | tf_op jit(solution)/shard_map/all_to_all | solution.py:119
  340.2 10.8 %all-to-all-start.2 = ((bf16[8,128,96]{1,2,0:T(8,128)(2,1)}), bf16[8,128,96]{1,2,0:T(8,128)(2,1)}, u32[]{:S(2)}, u32[]{:S(2)}) async-start(bf16[8,128,96]{1,2,0:T(8,128)(2,1)} %copy.101), calls=%async_computation.2 | async-start | bytes 393216 | tf_op jit(solution)/shard_map/all_to_all | solution.py:135
  345.1 93.8 %reduce-scatter.4.cloned.1.call-start = ((), (), s32[]{:S(2)}) async-start(), calls=%async_computation.9 | async-start | bytes 1671168 | tf_op jit(solution)/shard_map/reduce_scatter | solution.py:153
  359.6 6.6 collective-permute-start.7
  364.2 5.0 collective-permute-start.6
  371.0 191.8 %reduce-scatter.6.cloned.1.call-start = ((), (), s32[]{:S(2)}) async-start(), calls=%async_computation.10 | async-start | bytes 1671168 | tf_op jit(solution)/shard_map/reduce_scatter | solution.py:153
  473.0 16.2 %collective-permute-start.9 = (bf16[96,16]{1,0:T(8,128)(2,1)S(1)}, bf16[96,16]{1,0:T(8,128)(2,1)S(1)}, u32[]{:S(2)}, u32[]{:S(2)}) collective-permute-start(bf16[96,16]{1,0:T(8,128)(2,1)S(1)} %get-tuple-element.32), channel_id=1, source_target_pairs={{0,16},{16,32},{32,48},{48,64},{64,80},{80,96},{96,112},{1,17},{17... | collective-permute-start | bytes 9224 | tf_op jit(solution)/shard_map/ppermute | solution.py:23
  487.3 5.1 collective-permute-start.8
  494.3 178.4 %all-reduce.4.cloned.1.call-start = ((), (), s32[]{:S(2)}) async-start(), calls=%async_computation.12 | async-start | bytes 5308416 | tf_op jit(solution)/shard_map/psum | solution.py:168
  601.2 149.0 %reduce-scatter.8.cloned.1.call-start = ((), (), s32[]{:S(2)}) async-start(), calls=%async_computation.11 | async-start | bytes 1671168 | tf_op jit(solution)/shard_map/reduce_scatter | solution.py:153
  601.3 15.2 %collective-permute-start.11 = (bf16[96,8]{1,0:T(8,128)(2,1)S(1)}, bf16[96,8]{1,0:T(8,128)(2,1)S(1)}, u32[]{:S(2)}, u32[]{:S(2)}) collective-permute-start(bf16[96,8]{1,0:T(8,128)(2,1)S(1)} %get-tuple-element.30), channel_id=1, source_target_pairs={{0,16},{16,32},{32,48},{48,64},{64,80},{80,96},{96,112},{1,17},{17... | collective-permute-start | bytes 4616 | tf_op jit(solution)/shard_map/ppermute | solution.py:23
  614.6 5.6 collective-permute-start.10
  (31 other events, 1308.5 us)
Sparse Core Ops, SparseCore 0:
  63.0 39.3 all-gather.3
  157.6 38.6 all-gather.5
  250.8 38.6 all-gather.7
  371.1 67.7 reduce-scatter.3
  494.4 68.3 reduce-scatter.5
  601.3 71.2 all-reduce.3
  675.9 74.2 reduce-scatter.7
where the time goes:
time: 816 us; the launch traced here: 806 us
  waiting for transfers between devices  357 us (44%)
  blocking collectives  204 us (25%)
  starting transfers between devices  89.4 us (11%)
  local copies, waits for them, and re-layouts  71.9 us (9%)
  matrix products  35.4 us (4%)
  other arithmetic  33.8 us (4%)
  between operations  14.9 us (2%)
    reduce_scatter x3, waiting for transfers between devices, local(): lax.psum_scatter(term_rows(jnp.int32(0), local_ch * lax.axis_size('tp'))....  201 us
    psum x3, blocking collectives, local(): power = lax.psum(jnp.sum(stream * stream, axis=0), 'tp') / CHANNELS  96.2 us
    all_gather x3, waiting for transfers between devices, local(): lax.all_gather(padded, 'tp', axis=0, tiled=True)  75.1 us
    ppermute x6, starting transfers between devices, with_halo(): before = lax.ppermute(last, axis, up)  64.6 us
    psum x2, blocking collectives, local(): inner = lax.psum(jnp.sum(back_norm * stream, axis=0), 'tp')  62 us
    psum x1, waiting for transfers between devices, local(): lax.psum(weight_term.astype(jnp.bfloat16), 'seq').astype(jnp.float32)  50.6 us
    scatter x1, local copies, waits for them, and re-layouts, local(): jnp.zeros((seq_count, CAP), jnp.int32).at[owner, slot].set(acceptor_offset)  38.6 us
    psum x1, blocking collectives, local(): scores = lax.psum(partial_scores, 'tp')  31.4 us
  transfers between devices with their start and end apart: 22, of which 15 were waited for; matrix products, arithmetic and copies ran while one was open for 8% of the time, Pallas kernels for 0%

commit v1 on v0

--- a/solution.py
+++ b/solution.py
@@ -1,16 +1,268 @@
 import math
+import functools
 
 import jax
 import jax.numpy as jnp
 from jax import lax
+from jax.experimental import pallas as pl
+from jax.experimental.pallas import tpu as pltpu
 from jax.sharding import PartitionSpec as P
 
 CHANNELS = 1536
 LAYERS = 3
 CAP = 128
+WIN = 640
+SIDE = 4
+MESH = pl.DeviceIdType.MESH
 
 
 EPSILON = 1e-06
+
+
+def remote(src, dst, send_sem, recv_sem, device):
+    return pltpu.make_async_remote_copy(
+        src_ref=src,
+        dst_ref=dst,
+        send_sem=send_sem,
+        recv_sem=recv_sem,
+        device_id=device,
+        device_id_type=MESH,
+    )
+
+
+def forward_kernel(
+    seq_ref,
+    w_ref,
+    gain_ref,
+    hid_ref,
+    states_ref,
+    inv_ref,
+    gst,
+    halo_rx,
+    halo_send,
+    halo_recv,
+    send_sems,
+    recv_sems,
+):
+    seq_count = lax.axis_size("seq")
+    s = lax.axis_index("seq")
+    me = lax.axis_index("tp")
+    mx = me // SIDE
+    my = lax.rem(me, SIDE)
+
+    def xpeer(d):
+        return lax.rem(mx + d, SIDE) * SIDE + my
+
+    def ypeer(d):
+        return mx * SIDE + lax.rem(my + d, SIDE)
+
+    barrier = pltpu.get_barrier_semaphore()
+    for d in range(1, SIDE):
+        pl.semaphore_signal(barrier, inc=1, device_id={"tp": xpeer(d)}, device_id_type=MESH)
+        pl.semaphore_signal(barrier, inc=1, device_id={"tp": ypeer(d)}, device_id_type=MESH)
+
+    @pl.when(s > 0)
+    def _():
+        pl.semaphore_signal(barrier, inc=1, device_id={"seq": s - 1}, device_id_type=MESH)
+
+    @pl.when(s < seq_count - 1)
+    def _():
+        pl.semaphore_signal(barrier, inc=1, device_id={"seq": s + 1}, device_id_type=MESH)
+
+    sides = jnp.where(s > 0, 1, 0) + jnp.where(s < seq_count - 1, 1, 0)
+    pl.semaphore_wait(barrier, 2 * (SIDE - 1) + sides)
+
+    def to_left():
+        return remote(
+            seq_ref.at[:, 0:128], halo_rx.at[0], halo_send.at[0], halo_recv.at[0], {"seq": s - 1}
+        )
+
+    def to_right():
+        return remote(
+            seq_ref.at[:, 384:512], halo_rx.at[1], halo_send.at[1], halo_recv.at[1], {"seq": s + 1}
+        )
+
+    @pl.when(s > 0)
+    def _():
+        to_left().start()
+
+    @pl.when(s < seq_count - 1)
+    def _():
+        to_right().start()
+
+    @pl.when(s == 0)
+    def _():
+        halo_rx[1] = jnp.zeros((96, 128), jnp.bfloat16)
+
+    @pl.when(s == seq_count - 1)
+    def _():
+        halo_rx[0] = jnp.zeros((96, 128), jnp.bfloat16)
+
+    lane = lax.broadcasted_iota(jnp.int32, (96, 128), 1)
+    gain = gain_ref[...]
+    high = gain.astype(jnp.bfloat16).astype(jnp.float32)
+    rest = gain - high
+    mid = rest.astype(jnp.bfloat16).astype(jnp.float32)
+    low = rest - mid
+    packed = jnp.where(lane < 59, high, jnp.where(lane < 62, mid, low))
+    in_gain = (lane >= 56) & (lane < 65)
+
+    for h in range(2):
+        gst[0, me, h, :, 0:512] = seq_ref[48 * h : 48 * h + 48, :]
+
+    @pl.when(s > 0)
+    def _():
+        to_left().wait_send()
+        remote(
+            seq_ref.at[:, 384:512], halo_rx.at[1], halo_send.at[1], halo_recv.at[1], {"seq": s - 1}
+        ).wait_recv()
+
+    @pl.when(s < seq_count - 1)
+    def _():
+        to_right().wait_send()
+        remote(
+            seq_ref.at[:, 0:128], halo_rx.at[0], halo_send.at[0], halo_recv.at[0], {"seq": s + 1}
+        ).wait_recv()
+
+    halo = jnp.where(
+        lane < 64, halo_rx[0].astype(jnp.float32), halo_rx[1].astype(jnp.float32)
+    )
+    tile = jnp.where(in_gain, packed, halo).astype(jnp.bfloat16)
+    for h in range(2):
+        gst[0, me, h, :, 512:640] = tile[48 * h : 48 * h + 48, :]
+
+    col = lax.broadcasted_iota(jnp.int32, (96, WIN), 1)
+    outside = ((s == seq_count - 1) & (col >= 512) & (col < 576)) | ((s == 0) & (col >= 576))
+
+    for layer in range(LAYERS):
+        reach = 2 ** (layer + 3)
+
+        def send(slot, block, h, peer, layer=layer):
+            return remote(
+                gst.at[layer, block, h],
+                gst.at[layer, block, h],
+                send_sems.at[slot],
+                recv_sems.at[layer, block, h],
+                {"tp": peer},
+            )
+
+        def arrived(block, h, layer=layer):
+            remote(
+                gst.at[layer, block, h],
+                gst.at[layer, block, h],
+                send_sems.at[0],
+                recv_sems.at[layer, block, h],
+                {"tp": xpeer(1)},
+            ).wait_recv()
+
+        sent = []
+
+        def go(block, h, peer):
+            copy = send(len(sent), block, h, peer)
+            copy.start()
+            sent.append(copy)
+
+        for d in (1, 3, 2):
+            go(me, 0, xpeer(d))
+            go(me, 1, ypeer(d))
+        for d in (1, 3, 2):
+            go(me, 0, ypeer(d))
+            go(me, 1, xpeer(d))
+
+        def square(block, h, layer=layer):
+            x = gst[layer, block, h].astype(jnp.float32)
+            return jnp.sum((x * x).reshape(6, 8, WIN), axis=0)
+
+        total = square(me, 0) + square(me, 1)
+        for d in (1, 3, 2):
+            arrived(xpeer(d), 0)
+            for e in (1, 3, 2):
+                go(xpeer(d), 0, ypeer(e))
+            arrived(ypeer(d), 1)
+            for e in (1, 3, 2):
+                go(ypeer(d), 1, xpeer(e))
+            total = total + square(xpeer(d), 0) + square(ypeer(d), 1)
+        for d in (1, 3, 2):
+            arrived(xpeer(d), 1)
+            arrived(ypeer(d), 0)
+            total = total + square(xpeer(d), 1) + square(ypeer(d), 0)
+        for d in (1, 3, 2):
+            for e in (1, 3, 2):
+                block = lax.rem(mx + d, SIDE) * SIDE + lax.rem(my + e, SIDE)
+                arrived(block, 0)
+                arrived(block, 1)
+                total = total + square(block, 0) + square(block, 1)
+        power = jnp.sum(total, axis=0, keepdims=True) / CHANNELS
+        inverse = 1.0 / jnp.sqrt(power + EPSILON)
+        inv_ref[layer] = jnp.broadcast_to(inverse, (8, WIN))
+
+        def hide(block, carry, layer=layer):
+            inv = inv_ref[layer, 0:1, :]
+            for h in range(2):
+                head = gst[0, block, h, :, 512:640].astype(jnp.float32)
+                g = (
+                    head[:, 56 + layer : 57 + layer]
+                    + head[:, 59 + layer : 60 + layer]
+                    + head[:, 62 + layer : 63 + layer]
+                )
+                x = gst[layer, block, h].astype(jnp.float32) * inv * g
+                inner = x + 0.044715 * (x * x * x)
+                y = 0.5 * x * (1.0 + jnp.tanh(math.sqrt(2.0 / math.pi) * inner))
+                rows = pl.ds(pl.multiple_of(block * 96 + 48 * h, 16), 48)
+                hid_ref[layer, rows, :] = y.astype(jnp.bfloat16)
+            return carry
+
+        lax.fori_loop(0, SIDE * SIDE, hide, 0)
+
+        parts = []
+        for start, width in ((0, 256), (256, 256), (512, 128)):
+            parts.append(
+                jnp.dot(
+                    w_ref[layer],
+                    hid_ref[layer, :, start : start + width],
+                    preferred_element_type=jnp.float32,
+                )
+            )
+        y = jnp.concatenate(parts, axis=1)
+        mixed = (
+            pltpu.roll(y[0:96], reach, 1) + y[96:192] + pltpu.roll(y[192:288], WIN - reach, 1)
+        )
+        own = jnp.concatenate([gst[layer, me, 0], gst[layer, me, 1]], axis=0)
+        state = own.astype(jnp.float32) + mixed
+        if layer < LAYERS - 1:
+            state = jnp.where(outside, 0.0, state).astype(jnp.bfloat16)
+            for h in range(2):
+                gst[layer + 1, me, h] = state[48 * h : 48 * h + 48, :]
+        else:
+            state = state.astype(jnp.bfloat16)
+        states_ref[layer] = state[:, 0:512]
+        for copy in sent:
+            copy.wait_send()
+
+
+def forward(sequence_in, weights, gain_tile):
+    return pl.pallas_call(
+        forward_kernel,
+        out_shape=(
+            jax.ShapeDtypeStruct((LAYERS, CHANNELS, WIN), jnp.bfloat16),
+            jax.ShapeDtypeStruct((LAYERS, 96, 512), jnp.bfloat16),
+            jax.ShapeDtypeStruct((LAYERS, 8, WIN), jnp.float32),
+        ),
+        in_specs=[pl.BlockSpec(memory_space=pltpu.VMEM)] * 3,
+        out_specs=(pl.BlockSpec(memory_space=pltpu.VMEM),) * 3,
+        scratch_shapes=[
+            pltpu.VMEM((LAYERS, 16, 2, 48, WIN), jnp.bfloat16),
+            pltpu.VMEM((2, 96, 128), jnp.bfloat16),
+            pltpu.SemaphoreType.DMA((2,)),
+            pltpu.SemaphoreType.DMA((2,)),
+            pltpu.SemaphoreType.DMA((30,)),
+            pltpu.SemaphoreType.DMA((LAYERS, 16, 2)),
+        ],
+        compiler_params=pltpu.CompilerParams(
+            collective_id=0, has_side_effects=True, vmem_limit_bytes=56 * 1024 * 1024
+        ),
+        name="forward_section",
+    )(sequence_in, weights, gain_tile)
 
 
 def with_halo(x, sides, width):
@@ -86,29 +338,19 @@
     local_ch = sequence_in.shape[0]
     length = sequence_in.shape[1]
     seq_count = lax.axis_size("seq")
-    state = sequence_in
+    gain_tile = jnp.pad(jnp.tile(norm_gain.T, (1, 3)), ((0, 0), (56, 63)))
+    stacked = conv_weight.transpose(0, 2, 1, 3).reshape(LAYERS, 3 * local_ch, CHANNELS)
+    hidden_all, states, inverses = forward(sequence_in, stacked, gain_tile)
     stored = []
     for layer in range(LAYERS):
         reach = 2 ** (layer + 3)
-        stream = state.astype(jnp.float32)
-        power = lax.psum(jnp.sum(stream * stream, axis=0), "tp") / CHANNELS
-        inverse = 1.0 / jnp.sqrt(power + EPSILON)
-        pre_act = stream * inverse[None, :] * norm_gain[layer][:, None]
-        hidden = gelu_fn(pre_act).astype(jnp.bfloat16)
-        padded = widen(hidden, reach)
-        weights = conv_weight[layer]
-        gathered = padded
-
-        def fold_inputs(total, piece, start, weights=weights, reach=reach):
-            return forward_taps(weights, piece, reach, length)
-
-        mixed = fold_inputs(
-            jnp.zeros((local_ch, length), jnp.float32),
-            lax.all_gather(padded, "tp", axis=0, tiled=True),
-            jnp.int32(0),
-        )
+        state = sequence_in if layer == 0 else states[layer - 1]
+        inverse = inverses[layer, 0, :length]
+        pre_act = state.astype(jnp.float32) * inverse[None, :] * norm_gain[layer][:, None]
+        window = hidden_all[layer]
+        gathered = jnp.concatenate([window[:, WIN - reach :], window[:, : length + reach]], axis=1)
         stored.append((state, inverse, pre_act, gathered))
-        state = (stream + mixed).astype(jnp.bfloat16)
+    state = states[LAYERS - 1]
     owner = acceptor_owner[:, 0]
     member = (owner[:, None] == jnp.arange(seq_count, dtype=jnp.int32)[None, :]).astype(jnp.int32)
     slot = jnp.sum(jnp.cumsum(member, axis=0) * member, axis=1) - 1
@@ -162,7 +404,7 @@
 
         weight_term = fold_weights(
             jnp.zeros((local_ch, 3, CHANNELS), jnp.float32),
-            lax.all_gather(gathered, "tp", axis=0, tiled=True),
+            gathered,
             jnp.int32(0),
         )
         weight_list[layer] = lax.psum(weight_term.astype(jnp.bfloat16), "seq").astype(jnp.float32)

time: 816 us -> 643 us (0.79)
  blocking collectives: 204 us -> 108 us
  waiting for transfers between devices: 357 us -> 265 us
  Pallas kernels: 0 us -> 72.4 us
  starting transfers between devices: 89.4 us -> 52.4 us
  matrix products: 35.4 us -> 18.7 us
    psum x3 -> x0, blocking collectives: 96.2 us -> none  [local(): power = lax.psum(jnp.sum(stream * stream, axis=0), 'tp') / CHANNELS]
    all_gather x3 -> x0, waiting for transfers between devices: 75.1 us -> none  [local(): lax.all_gather(padded, 'tp', axis=0, tiled=True)]
    pallas_call x0 -> x1, Pallas kernels: none -> 72.4 us  [forward(): pl.pallas_call(forward_kernel, out_shape=(jax.ShapeDtypeStruct((LAYERS, C...]
    ppermute x6 -> x3, starting transfers between devices: 64.6 us -> 8.86 us  [with_halo(): before = lax.ppermute(last, axis, up)]
    ppermute x6 -> x3, waiting for transfers between devices: 17.5 us -> 0.01 us  [with_halo(): after = lax.ppermute(initial, axis, down)]
    ppermute x6 -> x3, starting transfers between devices: 11.5 us -> 25.8 us  [with_halo(): after = lax.ppermute(initial, axis, down)]
    dot_general x9 -> x0, matrix products: 13.4 us -> none  [forward_taps(): jnp.dot(weights[:, tap, :], padded[:, tap * reach:tap * reach + length],...]
  transfers between devices with their start and end apart: 22 -> 13, of which waited for: 15 -> 9; matrix products, arithmetic and copies ran while one was open for 8% -> 5% of each run, Pallas kernels for 0% -> 11%
where the time goes in v1:
time: 643 us; the launch traced here: 634 us
  waiting for transfers between devices  265 us (41%)
  blocking collectives  108 us (17%)
  Pallas kernels  72.4 us (11%)
  local copies, waits for them, and re-layouts  72 us (11%)
  starting transfers between devices  52.4 us (8%)
  other arithmetic  31 us (5%)
  matrix products  18.7 us (3%)
  between operations  14.4 us (2%)
    reduce_scatter x3, waiting for transfers between devices, local(): lax.psum_scatter(term_rows(jnp.int32(0), local_ch * lax.axis_size('tp'))....  201 us
    pallas_call x1, Pallas kernels, forward(): pl.pallas_call(forward_kernel, out_shape=(jax.ShapeDtypeStruct((LAYERS, C...  72.4 us
    psum x2, blocking collectives, local(): inner = lax.psum(jnp.sum(back_norm * stream, axis=0), 'tp')  61.9 us
    psum x1, waiting for transfers between devices, local(): lax.psum(weight_term.astype(jnp.bfloat16), 'seq').astype(jnp.float32)  53.2 us
    scatter x1, local copies, waits for them, and re-layouts, local(): jnp.zeros((seq_count, CAP), jnp.int32).at[owner, slot].set(acceptor_offset)  38.5 us
    psum x1, blocking collectives, local(): scores = lax.psum(partial_scores, 'tp')  31.4 us
    ppermute x3, starting transfers between devices, with_halo(): after = lax.ppermute(initial, axis, down)  25.8 us
    psum x1, blocking collectives, local(): gain_grad = lax.psum(jnp.stack(gain_list), 'seq')  14.8 us
  transfers between devices with their start and end apart: 13, of which 9 were waited for; matrix products, arithmetic and copies ran while one was open for 5% of the time, Pallas kernels for 11%

profile of v1, /device:TPU:1, one launch (start us, length us, event | category | flops | bytes accessed | tf_op | source)
XLA Modules:
  0.0 633.8 jit_solution(15632591852634090002)
XLA Ops:
  10.9 38.5 %scatter_fusion = s32[8,128]{1,0:T(8,128)} fusion(s32[8,128]{1,0:T(8,128)} %broadcast.133, s32[256]{0:T(256)S(1)} %bitcast.152, s32[256]{0:T(256)} %param.16), kind=kCustom, calls=%fused_computation.3 | custom fusion | bytes 5120 | tf_op jit(solution)/shard_map/scatter | solution.py:357
  49.5 6.8 %all-to-all-start = ((s32[8,1,128]{2,1,0:T(1,128)}), s32[8,1,128]{2,1,0:T(1,128)S(1)}, u32[]{:S(2)}, u32[]{:S(2)}) async-start(s32[8,1,128]{2,1,0:T(1,128)} %bitcast.14), calls=%async_computation | async-start | bytes 8192 | tf_op jit(solution)/shard_map/all_to_all | solution.py:359
  56.4 3.3 slice_bitcast_fusion.5
  60.4 72.4 %forward_section.1 = (bf16[3,1536,640]{2,1,0:T(8,128)(2,1)}, bf16[3,96,512]{2,1,0:T(8,128)(2,1)}, f32[3,8,640]{2,1,0:T(8,128)}) custom-call(bf16[96,512]{1,0:T(8,128)(2,1)} %seq_ref.1, bf16[3,288,1536]{2,1,0:T(8,128)(2,1)} %bitcast.155, f32[96,128]{1,0:T(8,128)} %pad.4.gain_ref), custom_call_target="tpu_custom_call" | custom-call | tf_op jit(solution)/shard_map/forward_section/pallas_call | solution.py:244
  135.0 3.2 gather_fusion.1
  139.1 6.6 %all-to-all-start.1 = ((bf16[8,128,96]{1,2,0:T(8,128)(2,1)}), bf16[8,128,96]{1,2,0:T(8,128)(2,1)S(1)}, u32[]{:S(2)}, u32[]{:S(2)}) async-start(bf16[8,128,96]{1,2,0:T(8,128)(2,1)} %copy.100), calls=%async_computation.1 | async-start | bytes 393216 | tf_op jit(solution)/shard_map/all_to_all | solution.py:361
  145.7 5.8 all-to-all-done.1
  154.7 12.4 %scatter_fusion.2 = f32[8,128,96]{2,1,0:T(8,128)S(1)} fusion(f32[8,128,96]{2,1,0:T(8,128)S(1)} %broadcast_in_dim.5, s32[256]{0:T(256)S(1)} %bitcast.153, f32[256,96]{1,0:T(8,128)S(1)} %copy.105), kind=kCustom, calls=%fused_computation.5 | custom fusion | bytes 296960 | tf_op jit(solution)/shard_map/scatter | solution.py:376
  167.8 4.2 all-to-all-start.2
  174.3 3.7 all-to-all-done.2
  178.9 7.8 %scatter_fusion.3 = f32[96,512]{0,1:T(8,128)S(1)} fusion(f32[96,512]{0,1:T(8,128)S(1)} %scatter_fusion.1, s32[1024]{0:T(1024)S(1)} %bitcast.172, f32[1024,96]{1,0:T(8,128)} %bitcast.159), kind=kCustom, calls=%fused_computation.6 | custom fusion | flops 98304 | bytes 1183744 | tf_op jit(solution)/shard_map/scatter-add | solution.py:381
  197.8 69.2 %reduce-scatter.4.cloned.1.call-done = bf16[96,512]{1,0:T(8,128)(2,1)} async-done(((bf16[1536,512]{1,0:T(8,128)(2,1)}), bf16[96,512]{1,0:T(8,128)(2,1)}) %reduce-scatter.4.cloned.1.call-update) | async-done | bytes 98320 | tf_op jit(solution)/shard_map/reduce_scatter | solution.py:395
  269.5 30.8 %psum.57 = f32[512]{0:T(512)S(1)} all-reduce(f32[512]{0:T(512)S(1)} %get-tuple-element.13), channel_id=1, replica_groups=mesh['seq'=8,'tp'=16] {'tp'}, use_global_device_ids=true, to_apply=%region_11.12 | all-reduce | flops 512 | bytes 4096 | tf_op jit(solution)/shard_map/psum | solution.py:415
  302.3 11.4 %collective-permute-start.2 = (bf16[96,16]{1,0:T(8,128)(2,1)S(1)}, bf16[96,16]{1,0:T(8,128)(2,1)S(1)}, u32[]{:S(2)}, u32[]{:S(2)}) collective-permute-start(bf16[96,16]{1,0:T(8,128)(2,1)S(1)} %get-tuple-element.40), channel_id=1, source_target_pairs={{16,0},{32,16},{48,32},{64,48},{80,64},{96,80},{112,96},{17,1},{33... | collective-permute-start | bytes 9224 | tf_op jit(solution)/shard_map/ppermute | solution.py:276
  320.4 3.2 slice_bitcast_fusion.2
  330.9 59.2 %reduce-scatter.6.cloned.1.call-done = bf16[96,512]{1,0:T(8,128)(2,1)} async-done(((bf16[1536,512]{1,0:T(8,128)(2,1)}), bf16[96,512]{1,0:T(8,128)(2,1)}) %reduce-scatter.6.cloned.1.call-update) | async-done | bytes 98320 | tf_op jit(solution)/shard_map/reduce_scatter | solution.py:395
  392.0 31.1 %psum.58 = f32[512]{0:T(512)S(1)} all-reduce(f32[512]{0:T(512)S(1)} %get-tuple-element.11), channel_id=1, replica_groups=mesh['seq'=8,'tp'=16] {'tp'}, use_global_device_ids=true, to_apply=%region_14.15 | all-reduce | flops 512 | bytes 4096 | tf_op jit(solution)/shard_map/psum | solution.py:415
  429.1 11.5 %collective-permute-start.4 = (bf16[96,8]{1,0:T(8,128)(2,1)S(1)}, bf16[96,8]{1,0:T(8,128)(2,1)S(1)}, u32[]{:S(2)}, u32[]{:S(2)}) collective-permute-start(bf16[96,8]{1,0:T(8,128)(2,1)S(1)} %get-tuple-element.38), channel_id=1, source_target_pairs={{16,0},{32,16},{48,32},{64,48},{80,64},{96,80},{112,96},{17,1},{33... | collective-permute-start | bytes 4616 | tf_op jit(solution)/shard_map/ppermute | solution.py:276
  440.6 3.1 collective-permute-start.5
  447.2 53.2 %all-reduce.5.cloned.1.call-done = (bf16[1,96,3,1536]{3,1,2,0:T(8,128)(2,1)}, bf16[1,96,3,1536]{3,1,2,0:T(8,128)(2,1)}, bf16[1,96,3,1536]{3,1,2,0:T(8,128)(2,1)}) async-done(((bf16[1,96,3,1536]{3,1,2,0:T(8,128)(2,1)}, bf16[1,96,3,1536]{3,1,2,0:T(8,128)(2,1)}, bf16[1,96,3,1536]{3,1,2,0:T(8,128)(2,1)}), (bf16[1,96,3,1536]{3,1,2,0:T(8,128)(2,1)}, bf16[1,96,3,1536]{3,1,2,0:T(8,128)(2,1)}, ...) | async-done | bytes 2654224 | tf_op jit(solution)/shard_map/psum | solution.py:410
  500.5 4.6 maximum_convert_fusion
  505.0 72.9 %reduce-scatter.8.cloned.1.call-done = bf16[96,512]{1,0:T(8,128)(2,1)} async-done(((bf16[1536,512]{1,0:T(8,128)(2,1)}), bf16[96,512]{1,0:T(8,128)(2,1)}) %reduce-scatter.8.cloned.1.call-update) | async-done | bytes 98320 | tf_op jit(solution)/shard_map/reduce_scatter | solution.py:395
  579.2 14.8 %psum.63 = f32[3,96]{1,0:T(4,128)} all-reduce(f32[3,96]{1,0:T(4,128)S(1)} %pad_maximum_fusion.18), channel_id=1, replica_groups=mesh['seq'=8,'tp'=16] {'seq'}, use_global_device_ids=true, to_apply=%region_24.25 | all-reduce | flops 288 | bytes 2304 | tf_op jit(solution)/shard_map/psum | solution.py:421
  593.9 31.4 %all-reduce.1 = (f32[256]{0:T(256)}, f32[512]{0:T(512)S(1)}) all-reduce(f32[256]{0:T(256)S(1)} %broadcast_multiply_fusion.1, f32[512]{0:T(512)S(1)} %get-tuple-element.15), channel_id=1, replica_groups=mesh['seq'=8,'tp'=16] {'tp'}, use_global_device_ids=true, to_apply=%region_5.6 | all-reduce | flops 768 | bytes 6144 | tf_op jit(solution)/shard_map/psum | solution.py:372
  (136 shorter events, 58.2 us)
Async XLA Ops:
  7.2 146.3 %copy-start = (f32[367,1536]{1,0:T(8,128)S(1)}, f32[367,1536]{1,0:T(8,128)}, u32[]{:S(2)}) copy-start(f32[367,1536]{1,0:T(8,128)} %param.13) | copy-start | bytes 6764548
  49.5 85.5 %all-to-all-start = ((s32[8,1,128]{2,1,0:T(1,128)}), s32[8,1,128]{2,1,0:T(1,128)S(1)}, u32[]{:S(2)}, u32[]{:S(2)}) async-start(s32[8,1,128]{2,1,0:T(1,128)} %bitcast.14), calls=%async_computation | async-start | bytes 8192 | tf_op jit(solution)/shard_map/all_to_all | solution.py:359
  59.7 74.1 %copy-start.10 = (f32[96,512]{1,0:T(8,128)S(1)}, f32[96,512]{1,0:T(8,128)}, u32[]{:S(2)}) copy-start(f32[96,512]{1,0:T(8,128)} %param.18) | copy-start | bytes 589828
  139.1 12.4 %all-to-all-start.1 = ((bf16[8,128,96]{1,2,0:T(8,128)(2,1)}), bf16[8,128,96]{1,2,0:T(8,128)(2,1)S(1)}, u32[]{:S(2)}, u32[]{:S(2)}) async-start(bf16[8,128,96]{1,2,0:T(8,128)(2,1)} %copy.100), calls=%async_computation.1 | async-start | bytes 393216 | tf_op jit(solution)/shard_map/all_to_all | solution.py:361
  167.8 10.1 %all-to-all-start.2 = ((bf16[8,128,96]{1,2,0:T(8,128)(2,1)}), bf16[8,128,96]{1,2,0:T(8,128)(2,1)S(1)}, u32[]{:S(2)}, u32[]{:S(2)}) async-start(bf16[8,128,96]{1,2,0:T(8,128)(2,1)} %copy.106), calls=%async_computation.2 | async-start | bytes 393216 | tf_op jit(solution)/shard_map/all_to_all | solution.py:377
  172.1 94.9 %reduce-scatter.4.cloned.1.call-start = ((), (), s32[]{:S(2)}) async-start(), calls=%async_computation.6 | async-start | bytes 1671168 | tf_op jit(solution)/shard_map/reduce_scatter | solution.py:395
  186.8 7.0 %collective-permute-start = (bf16[96,32]{0,1:T(8,128)(2,1)S(1)}, bf16[96,32]{0,1:T(8,128)(2,1)S(1)}, u32[]{:S(2)}, u32[]{:S(2)}) collective-permute-start(bf16[96,32]{0,1:T(8,128)(2,1)S(1)} %get-tuple-element.36), channel_id=1, source_target_pairs={{16,0},{32,16},{48,32},{64,48},{80,64},{96,80},{112,96},{17,1},{33... | collective-permute-start | bytes 18440 | tf_op jit(solution)/shard_map/ppermute | solution.py:276
  189.7 3.5 collective-permute-start.1
  195.6 121.3 %copy-start.4 = (bf16[96,3,1536]{2,0,1:T(8,128)(2,1)S(1)}, bf16[96,3,1536]{2,0,1:T(8,128)(2,1)}, u32[]{:S(2)}) copy-start(bf16[96,3,1536]{2,0,1:T(8,128)(2,1)} %get-tuple-element.32) | copy-start | bytes 2654212
  195.6 194.5 %reduce-scatter.6.cloned.1.call-start = ((), (), s32[]{:S(2)}) async-start(), calls=%async_computation.7 | async-start | bytes 1671168 | tf_op jit(solution)/shard_map/reduce_scatter | solution.py:395
  302.3 16.1 %collective-permute-start.2 = (bf16[96,16]{1,0:T(8,128)(2,1)S(1)}, bf16[96,16]{1,0:T(8,128)(2,1)S(1)}, u32[]{:S(2)}, u32[]{:S(2)}) collective-permute-start(bf16[96,16]{1,0:T(8,128)(2,1)S(1)} %get-tuple-element.40), channel_id=1, source_target_pairs={{16,0},{32,16},{48,32},{64,48},{80,64},{96,80},{112,96},{17,1},{33... | collective-permute-start | bytes 9224 | tf_op jit(solution)/shard_map/ppermute | solution.py:276
  313.8 4.0 collective-permute-start.3
  320.3 180.1 %all-reduce.5.cloned.1.call-start = ((), (), s32[]{:S(2)}) async-start(), calls=%async_computation.9 | async-start | bytes 5308416 | tf_op jit(solution)/shard_map/psum | solution.py:410
  329.3 60.8 %copy-start.11 = (f32[96]{0:T(128)S(1)}, f32[96]{0:T(128)}, u32[]{:S(2)}) copy-start(f32[96]{0:T(128)} %get-tuple-element.47) | copy-start | bytes 1156
  329.3 93.7 %copy-start.6 = (f32[96,512]{1,0:T(8,128)S(1)}, f32[96,512]{1,0:T(8,128)}, u32[]{:S(2)}) copy-start(f32[96,512]{1,0:T(8,128)} %get-tuple-element.23) | copy-start | bytes 589828
  429.0 148.9 %reduce-scatter.8.cloned.1.call-start = ((), (), s32[]{:S(2)}) async-start(), calls=%async_computation.8 | async-start | bytes 1671168 | tf_op jit(solution)/shard_map/reduce_scatter | solution.py:395
  429.1 16.2 %collective-permute-start.4 = (bf16[96,8]{1,0:T(8,128)(2,1)S(1)}, bf16[96,8]{1,0:T(8,128)(2,1)S(1)}, u32[]{:S(2)}, u32[]{:S(2)}) collective-permute-start(bf16[96,8]{1,0:T(8,128)(2,1)S(1)} %get-tuple-element.38), channel_id=1, source_target_pairs={{16,0},{32,16},{48,32},{64,48},{80,64},{96,80},{112,96},{17,1},{33... | collective-permute-start | bytes 4616 | tf_op jit(solution)/shard_map/ppermute | solution.py:276
  440.6 4.0 collective-permute-start.5
  500.5 77.4 %copy-start.9 = (bf16[96,512]{1,0:T(8,128)(2,1)S(1)}, bf16[96,512]{1,0:T(8,128)(2,1)}, u32[]{:S(2)}) copy-start(bf16[96,512]{1,0:T(8,128)(2,1)} %seq_ref.1) | copy-start | bytes 294916
  500.5 77.4 %copy-start.14 = (f32[96]{0:T(128)S(1)}, f32[96]{0:T(128)}, u32[]{:S(2)}) copy-start(f32[96]{0:T(128)} %get-tuple-element.46) | copy-start | bytes 1156
  500.5 78.7 %copy-start.16 = (f32[96]{0:T(128)S(1)}, f32[96]{0:T(128)}, u32[]{:S(2)}) copy-start(f32[96]{0:T(128)} %get-tuple-element.12) | copy-start | bytes 1156
  500.5 78.7 %copy-start.17 = (f32[96]{0:T(128)S(1)}, f32[96]{0:T(128)}, u32[]{:S(2)}) copy-start(f32[96]{0:T(128)} %get-tuple-element.10) | copy-start | bytes 1156
  500.5 124.9 %copy-start.8 = (f32[96,512]{1,0:T(8,128)S(1)}, f32[96,512]{1,0:T(8,128)}, u32[]{:S(2)}) copy-start(f32[96,512]{1,0:T(8,128)} %copy-done.7) | copy-start | bytes 589828
  500.5 124.9 %copy-start.12 = (f32[96]{0:T(128)S(1)}, f32[96]{0:T(128)}, u32[]{:S(2)}) copy-start(f32[96]{0:T(128)} %get-tuple-element.47) | copy-start | bytes 1156
  (10 other events, 199.5 us)
Sparse Core Ops, SparseCore 0:
  195.7 71.2 reduce-scatter.3
  320.4 69.6 reduce-scatter.5
  429.1 71.2 all-reduce.4
  503.5 74.3 reduce-scatter.7

commit v2 on v0

v2 whole, which is shorter than its diff:
```python
import math

import jax
import jax.numpy as jnp
from jax import lax
from jax.experimental import pallas as pl
from jax.experimental.pallas import tpu as pltpu
from jax.sharding import PartitionSpec as P

CHANNELS = 1536
LAYERS = 3
LOCAL = 96
HALF = 48
LENGTH = 512
WIN = 640
SIDE = 4
SEQ = 8
JUNC = 256
MESH = pl.DeviceIdType.MESH
EPSILON = 1e-06
ROOT = math.sqrt(CHANNELS)
GELU_C = math.sqrt(2.0 / math.pi)
GELU_A = 0.044715
F32 = jnp.float32
BF16 = jnp.bfloat16
NEAR = (1, 3, 2)


def remote(src, dst, send_sem, recv_sem, device):
    return pltpu.make_async_remote_copy(
        src_ref=src,
        dst_ref=dst,
        send_sem=send_sem,
        recv_sem=recv_sem,
        device_id=device,
        device_id_type=MESH,
    )


def dot(a, b):
    return jnp.dot(a, b, preferred_element_type=F32)


def dot_rows(a, b):
    return lax.dot_general(a, b, (((1,), (1,)), ((), ())), preferred_element_type=F32)


def section_kernel(
    seq_ref,
    w_ref,
    gain_ref,
    tower_ref,
    table_ref,
    meta_ref,
    donor_ref,
    tissue_ref,
    sgrad_ref,
    scores_ref,
    grad_ref,
    wgrad_ref,
    gains_ref,
    gst,
    hid,
    inv,
    wt,
    meta_all,
    pick,
    donor_hot,
    tissue_rows,
    state3,
    acc_tx,
    acc_rx,
    ab_tx,
    ab_rx,
    sc_all,
    up,
    gbuf,
    halo_rx,
    halo_b,
    pab,
    rx,
    sf,
    sab,
    ry,
    inn,
    wg,
    wrx,
    wz_tx,
    wz_rx,
    wres,
    gg,
    gg_all,
    halo_send,
    halo_recv,
    gather_send,
    gather_recv,
    meta_send,
    meta_recv,
    acc_send,
    acc_recv,
    ab_send,
    ab_recv,
    sc_send,
    sc_recv,
    rs_send,
    rs_recv,
    inn_send,
    inn_recv,
    w_send,
    w_recv,
    gg_send,
    gg_recv,
):
    s = lax.axis_index("seq")
    me = lax.axis_index("tp")
    mx = me // SIDE
    my = lax.rem(me, SIDE)
    mz = s // 2
    core = lax.rem(s, 2)

    def xpeer(d):
        return lax.rem(mx + d, SIDE) * SIDE + my

    def ypeer(d):
        return mx * SIDE + lax.rem(my + d, SIDE)

    def tpeer(d):
        return lax.rem(me + d, SIDE * SIDE)

    def speer(d):
        return lax.rem(s + d, SEQ)

    def zpeer(d):
        return lax.rem(mz + d, SIDE) * 2 + core

    partner = mz * 2 + 1 - core

    barrier = pltpu.get_barrier_semaphore()
    for d in range(1, SIDE * SIDE):
        pl.semaphore_signal(barrier, inc=1, device_id={"tp": tpeer(d)}, device_id_type=MESH)
    for d in range(1, SEQ):
        pl.semaphore_signal(barrier, inc=1, device_id={"seq": speer(d)}, device_id_type=MESH)
    pl.semaphore_wait(barrier, SIDE * SIDE - 1 + SEQ - 1)

    pending = []

    def begin(copy):
        copy.start()
        pending.append(copy)

    def halo_left(src, dst, k):
        return remote(src.at[:, 0:128], dst.at[0], halo_send.at[k, 0], halo_recv.at[k, 0], {"seq": s - 1})

    def halo_right(src, dst, k):
        return remote(src.at[:, 384:512], dst.at[1], halo_send.at[k, 1], halo_recv.at[k, 1], {"seq": s + 1})

    def halo_start(src, dst, k):
        @pl.when(s > 0)
        def _():
            halo_left(src, dst, k).start()

        @pl.when(s < SEQ - 1)
        def _():
            halo_right(src, dst, k).start()

        @pl.when(s == 0)
        def _():
            dst[1] = jnp.zeros((LOCAL, 128), BF16)

        @pl.when(s == SEQ - 1)
        def _():
            dst[0] = jnp.zeros((LOCAL, 128), BF16)

    def halo_wait(src, dst, k):
        @pl.when(s > 0)
        def _():
            halo_left(src, dst, k).wait_send()
            remote(
                src.at[:, 384:512], dst.at[1], halo_send.at[k, 1], halo_recv.at[k, 1], {"seq": s - 1}
            ).wait_recv()

        @pl.when(s < SEQ - 1)
        def _():
            halo_right(src, dst, k).wait_send()
            remote(
                src.at[:, 0:128], dst.at[0], halo_send.at[k, 0], halo_recv.at[k, 0], {"seq": s + 1}
            ).wait_recv()

    lane = lax.broadcasted_iota(jnp.int32, (LOCAL, 128), 1)

    def halo_tile(dst):
        return jnp.where(lane < 64, dst[0].astype(F32), dst[1].astype(F32))

    halo_start(seq_ref, halo_rx, 0)

    meta_all[s] = meta_ref[...]
    for d in range(1, SEQ):
        begin(
            remote(
                meta_all.at[s], meta_all.at[s], meta_send.at[d - 1], meta_recv.at[d - 1], {"seq": speer(d)}
            )
        )

    gain = gain_ref[...]
    high = gain.astype(BF16).astype(F32)
    rest = gain - high
    mid = rest.astype(BF16).astype(F32)
    low = rest - mid
    packed = jnp.where(lane < 59, high, jnp.where(lane < 62, mid, low))
    in_gain = (lane >= 56) & (lane < 65)

    for h in range(2):
        gst[0, me, h, :, 0:512] = seq_ref[HALF * h : HALF * h + HALF, :]
    halo_wait(seq_ref, halo_rx, 0)
    tile = jnp.where(in_gain, packed, halo_tile(halo_rx)).astype(BF16)
    for h in range(2):
        gst[0, me, h, :, 512:640] = tile[HALF * h : HALF * h + HALF, :]

    col = lax.broadcasted_iota(jnp.int32, (LOCAL, WIN), 1)
    outside = ((s == SEQ - 1) & (col >= 512) & (col < 576)) | ((s == 0) & (col >= 576))

    def transpose_weights(layer):
        for x in range(SIDE):
            block = w_ref[layer, :, 384 * x : 384 * x + 384].astype(F32).T.astype(BF16)
            for y in range(SIDE):
                a = 192 * x + HALF * y
                b = 768 + 192 * y + HALF * x
                wt[layer, a : a + HALF, :] = block[96 * y : 96 * y + HALF]
                wt[layer, b : b + HALF, :] = block[96 * y + HALF : 96 * y + 96]

    def one_hot(rows, row_ids, base):
        ids = lax.broadcasted_iota(jnp.int32, (rows, JUNC), 0) + base
        return jnp.where(ids == row_ids, 1.0, 0.0).astype(BF16)

    def prepare_tissues():
        table = table_ref[...]
        t_high = table.astype(BF16)
        t_rest = table - t_high.astype(F32)
        t_mid = t_rest.astype(BF16)
        t_low = (t_rest - t_mid.astype(F32)).astype(BF16)
        hot = one_hot(384, tissue_ref[...], 0)
        tissue_rows[...] = dot(t_high, hot) + dot(t_mid, hot) + dot(t_low, hot)
        donor_hot[...] = one_hot(LENGTH, donor_ref[...], 0)

    def prepare_picks():
        for d in range(1, SEQ):
            src = speer(SEQ - d)
            remote(
                meta_all.at[src], meta_all.at[src], meta_send.at[d - 1], meta_recv.at[d - 1], {"seq": src}
            ).wait_recv()
        for d in range(SEQ):
            pick[d] = one_hot(LENGTH, meta_all[speer(d)], s * LENGTH)

    for layer in range(LAYERS):
        reach = 2 ** (layer + 3)
        count = [0]

        def go(block, h, peer, layer=layer, count=count):
            begin(
                remote(
                    gst.at[layer, block, h],
                    gst.at[layer, block, h],
                    gather_send.at[layer, count[0]],
                    gather_recv.at[layer, block, h],
                    {"tp": peer},
                )
            )
            count[0] += 1

        def arrived(block, h, layer=layer):
            remote(
                gst.at[layer, block, h],
                gst.at[layer, block, h],
                gather_send.at[layer, 0],
                gather_recv.at[layer, block, h],
                {"tp": xpeer(1)},
            ).wait_recv()

        for d in NEAR:
            go(me, 0, xpeer(d))
            go(me, 1, ypeer(d))
        for d in NEAR:
            go(me, 0, ypeer(d))
            go(me, 1, xpeer(d))

        def square(block, h, layer=layer):
            x = gst[layer, block, h].astype(F32)
            return jnp.sum((x * x).reshape(6, 8, WIN), axis=0)

        total = square(me, 0) + square(me, 1)
        for d in NEAR:
            arrived(xpeer(d), 0)
            for e in NEAR:
                go(xpeer(d), 0, ypeer(e))
            arrived(ypeer(d), 1)
            for e in NEAR:
                go(ypeer(d), 1, xpeer(e))
            total = total + square(xpeer(d), 0) + square(ypeer(d), 1)

        transpose_weights(layer)
        if layer == 0:
            prepare_tissues()
        if layer == 1:
            prepare_picks()

        for d in NEAR:
            arrived(xpeer(d), 1)
            arrived(ypeer(d), 0)
            total = total + square(xpeer(d), 1) + square(ypeer(d), 0)
        for d in NEAR:
            for e in NEAR:
                block = lax.rem(mx + d, SIDE) * SIDE + lax.rem(my + e, SIDE)
                arrived(block, 0)
                arrived(block, 1)
                total = total + square(block, 0) + square(block, 1)
        power = jnp.sum(total, axis=0, keepdims=True) / CHANNELS
        inverse = 1.0 / jnp.sqrt(power + EPSILON)
        inv[layer] = jnp.broadcast_to(inverse, (8, WIN))

        def hide(block, carry, layer=layer):
            scale = inv[layer, 0:1, :]
            for h in range(2):
                head = gst[0, block, h, :, 512:640].astype(F32)
                g = (
                    head[:, 56 + layer : 57 + layer]
                    + head[:, 59 + layer : 60 + layer]
                    + head[:, 62 + layer : 63 + layer]
                )
                x = gst[layer, block, h].astype(F32) * scale * g
                t = jnp.tanh(GELU_C * (x + GELU_A * (x * x * x)))
                rows = pl.ds(pl.multiple_of(block * LOCAL + HALF * h, 16), HALF)
                hid[layer, rows, :] = (0.5 * x * (1.0 + t)).astype(BF16)
            return carry

        lax.fori_loop(0, SIDE * SIDE, hide, 0)

        parts = []
        for start, width in ((0, 256), (256, 256), (512, 128)):
            parts.append(dot(w_ref[layer], hid[layer, :, start : start + width]))
        y = jnp.concatenate(parts, axis=1)
        mixed = pltpu.roll(y[0:96], reach, 1) + y[96:192] + pltpu.roll(y[192:288], WIN - reach, 1)
        own = jnp.concatenate([gst[layer, me, 0], gst[layer, me, 1]], axis=0)
        state = own.astype(F32) + mixed
        if layer < LAYERS - 1:
            state = jnp.where(outside, 0.0, state).astype(BF16)
            for h in range(2):
                gst[layer + 1, me, h] = state[HALF * h : HALF * h + HALF, :]
        else:
            state3[...] = state[:, 0:LENGTH].astype(BF16)

    for d in range(1, SEQ):
        acc_tx[d - 1] = dot(state3[...], pick[d]).astype(BF16)
        begin(
            remote(
                acc_tx.at[d - 1], acc_rx.at[d - 1], acc_send.at[d - 1], acc_recv.at[d - 1], {"seq": speer(d)}
            )
        )
    accept = dot(state3[...], pick[0])
    donor = dot(state3[...], donor_hot[...])
    for d in range(1, SEQ):
        remote(
            acc_tx.at[d - 1], acc_rx.at[d - 1], acc_send.at[d - 1], acc_recv.at[d - 1], {"seq": speer(d)}
        ).wait_recv()
        accept = accept + acc_rx[d - 1].astype(F32)
    weight_j = sgrad_ref[...] / ROOT
    rows_q = tissue_rows[...]
    accept_back = (weight_j * donor * rows_q).astype(BF16)
    ab_tx[...] = accept_back
    for d in range(1, SEQ):
        begin(
            remote(ab_tx, ab_rx.at[d - 1], ab_send.at[d - 1], ab_recv.at[d - 1], {"seq": speer(d)})
        )
    sc_all[me] = jnp.sum(donor * accept * rows_q, axis=0, keepdims=True) / ROOT
    for d in range(1, SIDE * SIDE):
        begin(
            remote(sc_all.at[me], sc_all.at[me], sc_send.at[d - 1], sc_recv.at[d - 1], {"tp": tpeer(d)})
        )
    donor_back = weight_j * accept * rows_q
    d_high = donor_back.astype(BF16)
    d_low = (donor_back - d_high.astype(F32)).astype(BF16)
    added = (
        dot_rows(d_high, donor_hot[...])
        + dot_rows(d_low, donor_hot[...])
        + dot_rows(accept_back, pick[0])
    )
    up[...] = tower_ref[...] + added
    for d in range(1, SEQ):
        remote(
            ab_tx, ab_rx.at[d - 1], ab_send.at[d - 1], ab_recv.at[d - 1], {"seq": speer(d)}
        ).wait_recv()
        up[...] += dot_rows(ab_rx[d - 1], pick[SEQ - d])

    def w_cores(layer):
        return remote(
            wg.at[layer, 1 - core], wrx.at[layer], w_send.at[layer, 0], w_recv.at[layer, 0], {"seq": partner}
        )

    def w_slices(layer, d):
        return remote(
            wz_tx.at[layer, lax.rem(mz + d, SIDE)],
            wz_rx.at[layer, d - 1],
            w_send.at[layer, d],
            w_recv.at[layer, d],
            {"seq": zpeer(d)},
        )

    def w_result(layer, d):
        return remote(
            wres.at[layer, core, mz],
            wres.at[layer, core, mz],
            w_send.at[layer, 3 + d],
            w_recv.at[layer, 3 + d],
            {"seq": zpeer(d)},
        )

    def w_share(layer, d):
        part = wres.at[layer, core, lax.rem(mz + SIDE - d, SIDE)]
        return remote(part, part, w_send.at[layer, 7 + d], w_recv.at[layer, 7 + d], {"seq": partner})

    def w_step2(layer):
        w_cores(layer).wait_recv()
        summed = wg[layer, core].astype(F32) + wrx[layer].astype(F32)
        for q in range(SIDE):
            wz_tx[layer, q] = summed[:, 384 * q : 384 * q + 384].astype(BF16)
        for d in NEAR:
            begin(w_slices(layer, d))

    def w_step3(layer):
        result = wz_tx[layer, mz].astype(F32)
        for d in NEAR:
            w_slices(layer, d).wait_recv()
            result = result + wz_rx[layer, d - 1].astype(F32)
        wres[layer, core, mz] = result.astype(BF16)
        for d in NEAR:
            begin(w_result(layer, d))
        begin(w_share(layer, 0))

    def w_step4(layer):
        for d in NEAR:
            src = wres.at[layer, core, lax.rem(mz + SIDE - d, SIDE)]
            remote(
                src, src, w_send.at[layer, 3 + d], w_recv.at[layer, 3 + d], {"seq": zpeer(d)}
            ).wait_recv()
            begin(w_share(layer, d))

    def w_step5(layer):
        for d in range(SIDE):
            part = wres.at[layer, 1 - core, lax.rem(mz + SIDE - d, SIDE)]
            remote(
                part, part, w_send.at[layer, 7 + d], w_recv.at[layer, 7 + d], {"seq": partner}
            ).wait_recv()
        for h in range(2):
            for q in range(SIDE):
                wgrad_ref[layer, 144 * h : 144 * h + 144, 384 * q : 384 * q + 384] = wres[layer, h, q]

    gg[...] = jnp.zeros((128, 128), F32)
    for layer in reversed(range(LAYERS)):
        reach = 2 ** (layer + 3)
        shifts = (WIN - reach, 0, reach)
        gbuf[layer] = up[...].astype(BF16)
        halo_start(gbuf.at[layer], halo_b.at[layer], layer + 1)
        g = gbuf[layer].astype(F32)

        def shifted(window, shifts=shifts):
            rolled = [pltpu.roll(window, k, 1) if k else window for k in shifts]
            return jnp.concatenate(rolled, axis=0)

        inner_g = shifted(jnp.concatenate([g, jnp.zeros((LOCAL, 128), F32)], axis=1)).astype(BF16)
        for q in range(3):
            part = dot_rows(inner_g, hid[layer, 512 * q : 512 * q + 512, :]).astype(BF16)
            for h in range(2):
                wg[layer, h, :, 512 * q : 512 * q + 512] = part[144 * h : 144 * h + 144]
        begin(w_cores(layer))
        if layer < LAYERS - 1:
            w_step4(layer + 1)
        halo_wait(gbuf.at[layer], halo_b.at[layer], layer + 1)
        full_g = shifted(jnp.concatenate([g, halo_tile(halo_b.at[layer])], axis=1))
        full_g = full_g[:, 0:LENGTH].astype(BF16)

        def chunk(h, index, full_g=full_g, layer=layer):
            rows = pl.ds(pl.multiple_of(768 * h + 192 * index, 16), 192)
            return dot(wt[layer, rows, :], full_g)

        def rs_one(h, d, layer=layer):
            return remote(
                pab.at[layer, h, d - 1],
                rx.at[layer, h, d - 1],
                rs_send.at[layer, h, d - 1],
                rs_recv.at[layer, h, d - 1],
                {"tp": xpeer(d) if h == 0 else ypeer(d)},
            )

        def rs_two(h, d, layer=layer):
            index = lax.rem((my if h == 0 else mx) + d, SIDE)
            return remote(
                sab.at[layer, h, index],
                ry.at[layer, h, d - 1],
                rs_send.at[layer, h, 2 + d],
                rs_recv.at[layer, h, 2 + d],
                {"tp": ypeer(d) if h == 0 else xpeer(d)},
            )

        for d in NEAR:
            for h in range(2):
                base = mx if h == 0 else my
                pab[layer, h, d - 1] = chunk(h, lax.rem(base + d, SIDE)).astype(BF16)
                begin(rs_one(h, d))
        for h in range(2):
            sf[h] = chunk(h, mx if h == 0 else my).reshape(SIDE, HALF, LENGTH)
        w_step2(layer)
        for h in range(2):
            for d in NEAR:
                rs_one(h, d).wait_recv()
                sf[h] += rx[layer, h, d - 1].astype(F32).reshape(SIDE, HALF, LENGTH)
            sab[layer, h] = sf[h].astype(BF16)
            for d in NEAR:
                begin(rs_two(h, d))
        w_step3(layer)

        x = (seq_ref[...] if layer == 0 else jnp.concatenate(
            [gst[layer, me, 0, :, 0:LENGTH], gst[layer, me, 1, :, 0:LENGTH]], axis=0
        )).astype(F32)
        scale = inv[layer, 0:1, 0:LENGTH]
        g_col = gain_ref[:, 56 + layer : 57 + layer]
        norm = x * scale
        pre = norm * g_col
        t = jnp.tanh(GELU_C * (pre + GELU_A * (pre * pre * pre)))
        slope = 0.5 * (1.0 + t) + 0.5 * pre * (1.0 - t * t) * (
            GELU_C * (1.0 + 3.0 * GELU_A * (pre * pre))
        )
        halves = []
        for h in range(2):
            back = sf[h, my if h == 0 else mx]
            for d in NEAR:
                rs_two(h, d).wait_recv()
                back = back + ry[layer, h, d - 1].astype(F32)
            halves.append(back)
        back_pre = jnp.concatenate(halves, axis=0) * slope
        back_norm = back_pre * g_col
        inn[layer, me] = jnp.sum(back_norm * x, axis=0, keepdims=True)
        for d in range(1, SIDE * SIDE):
            begin(
                remote(
                    inn.at[layer, me],
                    inn.at[layer, me],
                    inn_send.at[layer, d - 1],
                    inn_recv.at[layer, d - 1],
                    {"tp": tpeer(d)},
                )
            )
        gain_col = jnp.sum(back_pre * norm, axis=1, keepdims=True)
        gg[0:LOCAL, :] = jnp.where(lane == layer, gain_col, gg[0:LOCAL, :])
        if layer == 0:
            gg_all[s] = gg[...].T[0:8]
            for d in range(1, SEQ):
                begin(
                    remote(
                        gg_all.at[s], gg_all.at[s], gg_send.at[d - 1], gg_recv.at[d - 1], {"seq": speer(d)}
                    )
                )
        for d in range(1, SIDE * SIDE):
            src = inn.at[layer, tpeer(SIDE * SIDE - d)]
            remote(
                src, src, inn_send.at[layer, d - 1], inn_recv.at[layer, d - 1], {"tp": tpeer(d)}
            ).wait_recv()
        inner = jnp.sum(inn[layer], axis=0)
        up[...] = up[...] + scale * back_norm - x * (scale * scale * scale) * (inner / CHANNELS)

    grad_ref[...] = up[...]
    w_step4(0)
    for d in range(1, SIDE * SIDE):
        src = sc_all.at[tpeer(SIDE * SIDE - d)]
        remote(src, src, sc_send.at[d - 1], sc_recv.at[d - 1], {"tp": tpeer(d)}).wait_recv()
    scores_ref[...] = jnp.sum(sc_all[...], axis=0)
    for d in range(1, SEQ):
        src = gg_all.at[speer(SEQ - d)]
        remote(src, src, gg_send.at[d - 1], gg_recv.at[d - 1], {"seq": speer(d)}).wait_recv()
    gains_ref[...] = jnp.sum(gg_all[...], axis=0)
    for layer in reversed(range(LAYERS)):
        w_step5(layer)
    for copy in pending:
        copy.wait_send()


def dma(*shape):
    return pltpu.SemaphoreType.DMA(shape)


def section(*operands):
    vmem = pl.BlockSpec(memory_space=pltpu.VMEM)
    return pl.pallas_call(
        section_kernel,
        out_shape=(
            jax.ShapeDtypeStruct((1, JUNC), F32),
            jax.ShapeDtypeStruct((LOCAL, LENGTH), F32),
            jax.ShapeDtypeStruct((LAYERS, 3 * LOCAL, CHANNELS), BF16),
            jax.ShapeDtypeStruct((8, 128), F32),
        ),
        in_specs=[vmem] * 9,
        out_specs=(vmem,) * 4,
        scratch_shapes=[
            pltpu.VMEM((LAYERS, 16, 2, HALF, WIN), BF16),
            pltpu.VMEM((LAYERS, CHANNELS, WIN), BF16),
            pltpu.VMEM((LAYERS, 8, WIN), F32),
            pltpu.VMEM((LAYERS, CHANNELS, 3 * LOCAL), BF16),
            pltpu.VMEM((SEQ, 1, JUNC), jnp.int32),
            pltpu.VMEM((SEQ, LENGTH, JUNC), BF16),
            pltpu.VMEM((LENGTH, JUNC), BF16),
            pltpu.VMEM((LOCAL, JUNC), F32),
            pltpu.VMEM((LOCAL, LENGTH), BF16),
            pltpu.VMEM((SEQ - 1, LOCAL, JUNC), BF16),
            pltpu.VMEM((SEQ - 1, LOCAL, JUNC), BF16),
            pltpu.VMEM((LOCAL, JUNC), BF16),
            pltpu.VMEM((SEQ - 1, LOCAL, JUNC), BF16),
            pltpu.VMEM((16, 1, JUNC), F32),
            pltpu.VMEM((LOCAL, LENGTH), F32),
            pltpu.VMEM((LAYERS, LOCAL, LENGTH), BF16),
            pltpu.VMEM((2, LOCAL, 128), BF16),
            pltpu.VMEM((LAYERS, 2, LOCAL, 128), BF16),
            pltpu.VMEM((LAYERS, 2, 3, 192, LENGTH), BF16),
            pltpu.VMEM((LAYERS, 2, 3, 192, LENGTH), BF16),
            pltpu.VMEM((2, SIDE, HALF, LENGTH), F32),
            pltpu.VMEM((LAYERS, 2, SIDE, HALF, LENGTH), BF16),
            pltpu.VMEM((LAYERS, 2, 3, HALF, LENGTH), BF16),
            pltpu.VMEM((LAYERS, 16, 1, LENGTH), F32),
            pltpu.VMEM((LAYERS, 2, 144, CHANNELS), BF16),
            pltpu.VMEM((LAYERS, 144, CHANNELS), BF16),
            pltpu.VMEM((LAYERS, SIDE, 144, 384), BF16),
            pltpu.VMEM((LAYERS, 3, 144, 384), BF16),
            pltpu.VMEM((LAYERS, 2, SIDE, 144, 384), BF16),
            pltpu.VMEM((128, 128), F32),
            pltpu.VMEM((SEQ, 8, 128), F32),
            dma(4, 2),
            dma(4, 2),
            dma(LAYERS, 30),
            dma(LAYERS, 16, 2),
            dma(7),
            dma(7),
            dma(7),
            dma(7),
            dma(7),
            dma(7),
            dma(15),
            dma(15),
            dma(LAYERS, 2, 6),
            dma(LAYERS, 2, 6),
            dma(LAYERS, 15),
            dma(LAYERS, 15),
            dma(LAYERS, 11),
            dma(LAYERS, 11),
            dma(7),
            dma(7),
        ],
        compiler_params=pltpu.CompilerParams(
            collective_id=0, has_side_effects=True, vmem_limit_bytes=62 * 1024 * 1024
        ),
        name="conv_section",
    )(*operands)


def local(
    sequence_in,
    conv_weight,
    norm_gain,
    tissue_scale,
    donor_offset,
    acceptor_owner,
    acceptor_offset,
    tissue,
    tower_grad,
    score_grad,
):
    gain_tile = jnp.pad(jnp.tile(norm_gain.T, (1, 3)), ((0, 0), (56, 63)))
    stacked = conv_weight.transpose(0, 2, 1, 3).reshape(LAYERS, 3 * LOCAL, CHANNELS)
    table = lax.dynamic_slice_in_dim(tissue_scale, lax.axis_index("tp") * LOCAL, LOCAL, 1).T
    table = jnp.pad(table, ((0, 0), (0, 384 - table.shape[1])))
    meta = (acceptor_owner[:, 0] * LENGTH + acceptor_offset)[None, :]
    scores, grad, weights, gains = section(
        sequence_in,
        stacked,
        gain_tile,
        tower_grad,
        table,
        meta,
        donor_offset[None, :],
        tissue[None, :],
        score_grad[None, :],
    )
    weights = weights.reshape(LAYERS, 3, LOCAL, CHANNELS).transpose(0, 2, 1, 3).astype(F32)
    return (scores[0], grad, weights, gains[:LAYERS, :LOCAL])


def solution(mesh):
    return jax.shard_map(
        local,
        mesh=mesh,
        in_specs=(
            P("tp", "seq"),
            P(None, "tp", None, None),
            P(None, "tp"),
            P(),
            P("seq"),
            P("seq", None),
            P("seq"),
            P("seq"),
            P("tp", "seq"),
            P("seq"),
        ),
        out_specs=(P("seq"), P("tp", "seq"), P(None, "tp", None, None), P(None, "tp")),
        check_vma=False,
    )
```

time: 816 us -> 178 us (0.22)
  waiting for transfers between devices: 357 us -> 0 us
  blocking collectives: 204 us -> 0 us
  Pallas kernels: 0 us -> 162 us
  starting transfers between devices: 89.4 us -> 0 us
  local copies, waits for them, and re-layouts: 71.9 us -> 5.9 us
  matrix products: 35.4 us -> 0 us
  other arithmetic: 33.8 us -> 6.82 us
  between operations: 14.9 us -> 0.66 us
    psum x7 -> x0, blocking collectives: 204 us -> none  [the longest x3 96.2 us: local(): power = lax.psum(jnp.sum(stream * stream, axis=0), 'tp') / CHANNELS]
    reduce_scatter x3 -> x0, waiting for transfers between devices: 201 us -> none  [local(): lax.psum_scatter(term_rows(jnp.int32(0), local_ch * lax.axis_size('tp'))....]
    pallas_call x0 -> x1, Pallas kernels: none -> 162 us  [section(): pl.pallas_call(section_kernel, out_shape=(jax.ShapeDtypeStruct((1, JUNC),...]
    ppermute x12 -> x0, starting transfers between devices: 76.1 us -> none  [the longest x6 64.6 us: with_halo(): before = lax.ppermute(last, axis, up)]
    all_gather x3 -> x0, waiting for transfers between devices: 75.1 us -> none  [local(): lax.all_gather(padded, 'tp', axis=0, tiled=True)]
    scatter x3 -> x0, local copies, waits for them, and re-layouts: 56.2 us -> none  [the longest x1 38.6 us: local(): jnp.zeros((seq_count, CAP), jnp.int32).at[owner, slot].set(acceptor_offset)]
    psum x1 -> x0, waiting for transfers between devices: 50.6 us -> none  [local(): lax.psum(weight_term.astype(jnp.bfloat16), 'seq').astype(jnp.float32)]
    dot_general x28 -> x0, matrix products: 35.4 us -> none  [the longest x9 13.4 us: forward_taps(): jnp.dot(weights[:, tap, :], padded[:, tap * reach:tap * reach + length],...]
  transfers between devices with their start and end apart: 22 -> 0, of which waited for: 15 -> 0; matrix products, arithmetic and copies ran while one was open for 8% -> 0% of each run, Pallas kernels for 0% -> 0%
where the time goes in v2:
time: 178 us; the launch traced here: 176 us
  Pallas kernels  162 us (91%)
  other arithmetic  6.82 us (4%)
  local copies, waits for them, and re-layouts  5.9 us (3%)
    pallas_call x1, Pallas kernels, section(): pl.pallas_call(section_kernel, out_shape=(jax.ShapeDtypeStruct((1, JUNC),...  162 us
    convert_element_type x1, other arithmetic, local(): weights.reshape(LAYERS, 3, LOCAL, CHANNELS).transpose(0, 2, 1, 3)  4.9 us

profile of v2, /device:TPU:1, one launch (start us, length us, event | category | flops | bytes accessed | tf_op | source)
XLA Modules:
  0.0 175.8 jit_solution(284297712603158339)
XLA Ops:
  0.6 0.7 broadcast_multiply_fusion
  1.3 1.2 add.11
  2.6 0.7 tile.4
  3.3 0.1 copy.16
  3.4 0.7 pad.8.gain_ref
  4.1 1.1 constant_dynamic-slice_fusion
  5.2 0.1 copy.18
  5.3 0.7 pad.9.table_ref
  6.0 162.5 %conv_section.1 = (f32[1,256]{1,0:T(1,128)}, f32[96,512]{1,0:T(8,128)}, bf16[3,288,1536]{2,1,0:T(8,128)(2,1)}, f32[8,128]{1,0:T(8,128)}) custom-call(bf16[96,512]{1,0:T(8,128)(2,1)} %seq_ref.1, bf16[3,288,1536]{2,1,0:T(8,128)(2,1)} %bitcast.17, f32[96,128]{1,0:T(8,128)} %pad.8.gain_ref, f32[96,512]{1,0:T(8,128)} %tower_ref.1, f32[96,384]{1,0:T(8,128)} %pad.9.table_ref, ...), custom_call_target="tpu_custom_call" | custom-call | tf_op jit(solution)/shard_map/conv_section/pallas_call | solution.py:591
  168.4 1.3 slice.3
  169.7 0.0 copy-start.1
  169.7 0.0 copy-start
  169.7 4.9 %convert_bitcast_fusion = f32[3,96,3,1536]{3,1,2,0:T(8,128)} fusion(bf16[3,3,96,1536]{3,2,1,0:T(8,128)(2,1)} %bitcast.18), kind=kLoop, calls=%fused_computation | loop fusion | flops 1327104 | bytes 7962624 | tf_op jit(solution)/shard_map/convert_element_type | solution.py:689
  174.6 0.0 copy-done.1
  174.6 0.6 copy.21
  175.2 0.0 copy-done
  175.2 0.7 copy.22
  (1 shorter events, 0.0 us)
Async XLA Ops:
  169.7 4.9 %copy-start.1 = (f32[1,256]{1,0:T(1,128)S(1)}, f32[1,256]{1,0:T(1,128)}, u32[]{:S(2)}) copy-start(f32[1,256]{1,0:T(1,128)} %get-tuple-element.8) | copy-start | bytes 3076
  169.7 5.5 %copy-start = (f32[96,512]{1,0:T(8,128)S(1)}, f32[96,512]{1,0:T(8,128)}, u32[]{:S(2)}) copy-start(f32[96,512]{1,0:T(8,128)} %get-tuple-element.17) | copy-start | bytes 589828

commit v3 on v2

--- a/solution.py
+++ b/solution.py
@@ -47,11 +47,12 @@
 
 def section_kernel(
     seq_ref,
-    w_ref,
-    gain_ref,
-    tower_ref,
+    w_hbm,
+    gain_in,
+    tower_hbm,
     table_ref,
-    meta_ref,
+    owner_ref,
+    offset_ref,
     donor_ref,
     tissue_ref,
     sgrad_ref,
@@ -59,8 +60,17 @@
     grad_ref,
     wgrad_ref,
     gains_ref,
+    w_ref,
+    tower_ref,
+    gain_ref,
+    turn,
+    tab,
     gst,
     hid,
+    mm,
+    vv,
+    ysum,
+    pw,
     inv,
     wt,
     meta_all,
@@ -110,6 +120,9 @@
     w_recv,
     gg_send,
     gg_recv,
+    pw_send,
+    pw_recv,
+    load_sem,
 ):
     s = lax.axis_index("seq")
     me = lax.axis_index("tp")
@@ -135,11 +148,20 @@
 
     partner = mz * 2 + 1 - core
 
+    load_w = pltpu.make_async_copy(w_hbm, w_ref, load_sem.at[0])
+    load_tower = pltpu.make_async_copy(tower_hbm, tower_ref, load_sem.at[1])
+    load_w.start()
+    load_tower.start()
+
     barrier = pltpu.get_barrier_semaphore()
     for d in range(1, SIDE * SIDE):
         pl.semaphore_signal(barrier, inc=1, device_id={"tp": tpeer(d)}, device_id_type=MESH)
     for d in range(1, SEQ):
         pl.semaphore_signal(barrier, inc=1, device_id={"seq": speer(d)}, device_id_type=MESH)
+    turn[...] = jnp.zeros((128, 128), F32)
+    for k in range(3):
+        turn[56 + 3 * k : 59 + 3 * k, 0:LOCAL] = gain_in[...]
+    gain_ref[...] = turn[...].T[0:LOCAL]
     pl.semaphore_wait(barrier, SIDE * SIDE - 1 + SEQ - 1)
 
     pending = []
@@ -193,7 +215,7 @@
 
     halo_start(seq_ref, halo_rx, 0)
 
-    meta_all[s] = meta_ref[...]
+    meta_all[s] = owner_ref[...] * LENGTH + offset_ref[...]
     for d in range(1, SEQ):
         begin(
             remote(
@@ -233,7 +255,9 @@
         return jnp.where(ids == row_ids, 1.0, 0.0).astype(BF16)
 
     def prepare_tissues():
-        table = table_ref[...]
+        tab[...] = jnp.zeros((384, 128), F32)
+        tab[0 : table_ref.shape[0], 0:LOCAL] = table_ref[...]
+        table = tab[...].T[0:LOCAL]
         t_high = table.astype(BF16)
         t_rest = table - t_high.astype(F32)
         t_mid = t_rest.astype(BF16)
@@ -276,6 +300,18 @@
                 {"tp": xpeer(1)},
             ).wait_recv()
 
+        squares = jnp.concatenate([gst[layer, me, 0], gst[layer, me, 1]], axis=0).astype(F32)
+        pw[layer, me] = jnp.sum(squares * squares, axis=0, keepdims=True)
+        for d in range(1, SIDE * SIDE):
+            begin(
+                remote(
+                    pw.at[layer, me],
+                    pw.at[layer, me],
+                    pw_send.at[layer, d - 1],
+                    pw_recv.at[layer, d - 1],
+                    {"tp": tpeer(d)},
+                )
+            )
         for d in NEAR:
             go(me, 0, xpeer(d))
             go(me, 1, ypeer(d))
@@ -283,11 +319,12 @@
             go(me, 0, ypeer(d))
             go(me, 1, xpeer(d))
 
-        def square(block, h, layer=layer):
-            x = gst[layer, block, h].astype(F32)
-            return jnp.sum((x * x).reshape(6, 8, WIN), axis=0)
-
-        total = square(me, 0) + square(me, 1)
+        if layer == 0:
+            prepare_tissues()
+            load_w.wait()
+        if layer > 0:
+            vv[layer - 1] = dot(w_ref[layer - 1], mm[layer - 1])
+
         for d in NEAR:
             arrived(xpeer(d), 0)
             for e in NEAR:
@@ -295,25 +332,13 @@
             arrived(ypeer(d), 1)
             for e in NEAR:
                 go(ypeer(d), 1, xpeer(e))
-            total = total + square(xpeer(d), 0) + square(ypeer(d), 1)
-
-        transpose_weights(layer)
-        if layer == 0:
-            prepare_tissues()
-        if layer == 1:
-            prepare_picks()
-
-        for d in NEAR:
-            arrived(xpeer(d), 1)
-            arrived(ypeer(d), 0)
-            total = total + square(xpeer(d), 1) + square(ypeer(d), 0)
-        for d in NEAR:
-            for e in NEAR:
-                block = lax.rem(mx + d, SIDE) * SIDE + lax.rem(my + e, SIDE)
-                arrived(block, 0)
-                arrived(block, 1)
-                total = total + square(block, 0) + square(block, 1)
-        power = jnp.sum(total, axis=0, keepdims=True) / CHANNELS
+
+        for d in range(1, SIDE * SIDE):
+            src = pw.at[layer, tpeer(SIDE * SIDE - d)]
+            remote(
+                src, src, pw_send.at[layer, d - 1], pw_recv.at[layer, d - 1], {"tp": tpeer(d)}
+            ).wait_recv()
+        power = jnp.sum(pw[layer], axis=0) / CHANNELS
         inverse = 1.0 / jnp.sqrt(power + EPSILON)
         inv[layer] = jnp.broadcast_to(inverse, (8, WIN))
 
@@ -326,18 +351,44 @@
                     + head[:, 59 + layer : 60 + layer]
                     + head[:, 62 + layer : 63 + layer]
                 )
-                x = gst[layer, block, h].astype(F32) * scale * g
+                rows = pl.ds(pl.multiple_of(block * LOCAL + HALF * h, 16), HALF)
+                raw = gst[layer, block, h, :, 0:LENGTH].astype(F32) * g
+                x = raw * scale[:, 0:LENGTH]
+                xx = x * x
+                t = jnp.tanh(GELU_C * (x + GELU_A * (xx * x)))
+                upper = 0.5 * (1.0 + t)
+                hid[layer, rows, 0:LENGTH] = (x * upper).astype(BF16)
+                slope = upper + (0.5 * x) * (1.0 - t * t) * (GELU_C + (3.0 * GELU_A * GELU_C) * xx)
+                mm[layer, rows, :] = (raw * slope).astype(BF16)
+                x = gst[layer, block, h, :, LENGTH:WIN].astype(F32) * scale[:, LENGTH:WIN] * g
                 t = jnp.tanh(GELU_C * (x + GELU_A * (x * x * x)))
-                rows = pl.ds(pl.multiple_of(block * LOCAL + HALF * h, 16), HALF)
-                hid[layer, rows, :] = (0.5 * x * (1.0 + t)).astype(BF16)
+                hid[layer, rows, LENGTH:WIN] = (0.5 * x * (1.0 + t)).astype(BF16)
             return carry
 
-        lax.fori_loop(0, SIDE * SIDE, hide, 0)
-
-        parts = []
-        for start, width in ((0, 256), (256, 256), (512, 128)):
-            parts.append(dot(w_ref[layer], hid[layer, :, start : start + width]))
-        y = jnp.concatenate(parts, axis=1)
+        for d in (0,) + NEAR:
+            group = lax.rem(mx + d, SIDE)
+            if d == 0:
+                for e in NEAR:
+                    arrived(ypeer(e), 0)
+            else:
+                arrived(xpeer(d), 1)
+                for e in NEAR:
+                    block = group * SIDE + lax.rem(my + e, SIDE)
+                    arrived(block, 0)
+                    arrived(block, 1)
+            lax.fori_loop(group * SIDE, group * SIDE + SIDE, hide, 0)
+            span = pl.ds(pl.multiple_of(group * 384, 128), 384)
+            part = dot(w_ref[layer, :, span], hid[layer, span, :])
+            if d == 0:
+                ysum[...] = part
+                transpose_weights(layer)
+                if layer == 1:
+                    prepare_picks()
+            elif d != NEAR[-1]:
+                ysum[...] += part
+            else:
+                y = ysum[...] + part
+
         mixed = pltpu.roll(y[0:96], reach, 1) + y[96:192] + pltpu.roll(y[192:288], WIN - reach, 1)
         own = jnp.concatenate([gst[layer, me, 0], gst[layer, me, 1]], axis=0)
         state = own.astype(F32) + mixed
@@ -355,6 +406,8 @@
                 acc_tx.at[d - 1], acc_rx.at[d - 1], acc_send.at[d - 1], acc_recv.at[d - 1], {"seq": speer(d)}
             )
         )
+    vv[LAYERS - 1] = dot(w_ref[LAYERS - 1], mm[LAYERS - 1])
+    load_tower.wait()
     accept = dot(state3[...], pick[0])
     donor = dot(state3[...], donor_hot[...])
     for d in range(1, SEQ):
@@ -475,7 +528,19 @@
             w_step4(layer + 1)
         halo_wait(gbuf.at[layer], halo_b.at[layer], layer + 1)
         full_g = shifted(jnp.concatenate([g, halo_tile(halo_b.at[layer])], axis=1))
-        full_g = full_g[:, 0:LENGTH].astype(BF16)
+        full_g = full_g[:, 0:LENGTH]
+        inn[layer, me] = jnp.sum(full_g * vv[layer], axis=0, keepdims=True)
+        for d in range(1, SIDE * SIDE):
+            begin(
+                remote(
+                    inn.at[layer, me],
+                    inn.at[layer, me],
+                    inn_send.at[layer, d - 1],
+                    inn_recv.at[layer, d - 1],
+                    {"tp": tpeer(d)},
+                )
+            )
+        full_g = full_g.astype(BF16)
 
         def chunk(h, index, full_g=full_g, layer=layer):
             rows = pl.ds(pl.multiple_of(768 * h + 192 * index, 16), 192)
@@ -515,7 +580,10 @@
             sab[layer, h] = sf[h].astype(BF16)
             for d in NEAR:
                 begin(rs_two(h, d))
-        w_step3(layer)
+            if h == 0 and layer == 0:
+                w_step3(layer)
+        if layer > 0:
+            w_step3(layer)
 
         x = (seq_ref[...] if layer == 0 else jnp.concatenate(
             [gst[layer, me, 0, :, 0:LENGTH], gst[layer, me, 1, :, 0:LENGTH]], axis=0
@@ -537,17 +605,6 @@
             halves.append(back)
         back_pre = jnp.concatenate(halves, axis=0) * slope
         back_norm = back_pre * g_col
-        inn[layer, me] = jnp.sum(back_norm * x, axis=0, keepdims=True)
-        for d in range(1, SIDE * SIDE):
-            begin(
-                remote(
-                    inn.at[layer, me],
-                    inn.at[layer, me],
-                    inn_send.at[layer, d - 1],
-                    inn_recv.at[layer, d - 1],
-                    {"tp": tpeer(d)},
-                )
-            )
         gain_col = jnp.sum(back_pre * norm, axis=1, keepdims=True)
         gg[0:LOCAL, :] = jnp.where(lane == layer, gain_col, gg[0:LOCAL, :])
         if layer == 0:
@@ -575,7 +632,7 @@
     for d in range(1, SEQ):
         src = gg_all.at[speer(SEQ - d)]
         remote(src, src, gg_send.at[d - 1], gg_recv.at[d - 1], {"seq": speer(d)}).wait_recv()
-    gains_ref[...] = jnp.sum(gg_all[...], axis=0)
+    gains_ref[...] = jnp.sum(gg_all[...], axis=0)[0:LAYERS, 0:LOCAL]
     for layer in reversed(range(LAYERS)):
         w_step5(layer)
     for copy in pending:
@@ -588,19 +645,29 @@
 
 def section(*operands):
     vmem = pl.BlockSpec(memory_space=pltpu.VMEM)
+    hbm = pl.BlockSpec(memory_space=pl.ANY)
     return pl.pallas_call(
         section_kernel,
         out_shape=(
             jax.ShapeDtypeStruct((1, JUNC), F32),
             jax.ShapeDtypeStruct((LOCAL, LENGTH), F32),
             jax.ShapeDtypeStruct((LAYERS, 3 * LOCAL, CHANNELS), BF16),
-            jax.ShapeDtypeStruct((8, 128), F32),
+            jax.ShapeDtypeStruct((LAYERS, LOCAL), F32),
         ),
-        in_specs=[vmem] * 9,
+        in_specs=[vmem, hbm, vmem, hbm] + [vmem] * 6,
         out_specs=(vmem,) * 4,
         scratch_shapes=[
+            pltpu.VMEM((LAYERS, 3 * LOCAL, CHANNELS), BF16),
+            pltpu.VMEM((LOCAL, LENGTH), F32),
+            pltpu.VMEM((LOCAL, 128), F32),
+            pltpu.VMEM((128, 128), F32),
+            pltpu.VMEM((384, 128), F32),
             pltpu.VMEM((LAYERS, 16, 2, HALF, WIN), BF16),
             pltpu.VMEM((LAYERS, CHANNELS, WIN), BF16),
+            pltpu.VMEM((LAYERS, CHANNELS, LENGTH), BF16),
+            pltpu.VMEM((LAYERS, 3 * LOCAL, LENGTH), F32),
+            pltpu.VMEM((3 * LOCAL, WIN), F32),
+            pltpu.VMEM((LAYERS, 16, 1, WIN), F32),
             pltpu.VMEM((LAYERS, 8, WIN), F32),
             pltpu.VMEM((LAYERS, CHANNELS, 3 * LOCAL), BF16),
             pltpu.VMEM((SEQ, 1, JUNC), jnp.int32),
@@ -650,6 +717,9 @@
             dma(LAYERS, 11),
             dma(7),
             dma(7),
+            dma(LAYERS, 15),
+            dma(LAYERS, 15),
+            dma(2),
         ],
         compiler_params=pltpu.CompilerParams(
             collective_id=0, has_side_effects=True, vmem_limit_bytes=62 * 1024 * 1024
@@ -670,24 +740,22 @@
     tower_grad,
     score_grad,
 ):
-    gain_tile = jnp.pad(jnp.tile(norm_gain.T, (1, 3)), ((0, 0), (56, 63)))
     stacked = conv_weight.transpose(0, 2, 1, 3).reshape(LAYERS, 3 * LOCAL, CHANNELS)
-    table = lax.dynamic_slice_in_dim(tissue_scale, lax.axis_index("tp") * LOCAL, LOCAL, 1).T
-    table = jnp.pad(table, ((0, 0), (0, 384 - table.shape[1])))
-    meta = (acceptor_owner[:, 0] * LENGTH + acceptor_offset)[None, :]
+    table = lax.dynamic_slice_in_dim(tissue_scale, lax.axis_index("tp") * LOCAL, LOCAL, 1)
     scores, grad, weights, gains = section(
         sequence_in,
         stacked,
-        gain_tile,
+        norm_gain,
         tower_grad,
         table,
-        meta,
+        acceptor_owner.T,
+        acceptor_offset[None, :],
         donor_offset[None, :],
         tissue[None, :],
         score_grad[None, :],
     )
     weights = weights.reshape(LAYERS, 3, LOCAL, CHANNELS).transpose(0, 2, 1, 3).astype(F32)
-    return (scores[0], grad, weights, gains[:LAYERS, :LOCAL])
+    return (scores[0], grad, weights, gains)
 
 
 def solution(mesh):

time: 178 us -> 163 us (0.916); the launches traced: 176 us -> 163 us
  Pallas kernels: 162 us -> 154 us
  local copies, waits for them, and re-layouts: 5.9 us -> 3.62 us
  other arithmetic: 6.82 us -> 4.9 us
    pallas_call x1, Pallas kernels: 162 us -> 154 us  [section(): pl.pallas_call(section_kernel, out_shape=(jax.ShapeDtypeStruct((1, JUNC),...]
where the time goes in v3:
time: 163 us
  Pallas kernels  154 us (94%)
  other arithmetic  4.9 us (3%)
  local copies, waits for them, and re-layouts  3.62 us (2%)
    pallas_call x1, Pallas kernels, section(): pl.pallas_call(section_kernel, out_shape=(jax.ShapeDtypeStruct((1, JUNC),...  154 us
    convert_element_type x1, other arithmetic, local(): weights.reshape(LAYERS, 3, LOCAL, CHANNELS).transpose(0, 2, 1, 3)  4.9 us

profile of v3, /device:TPU:1, one launch (start us, length us, event | category | flops | bytes accessed | tf_op | source)
XLA Modules:
  0.0 162.8 jit_solution(7901168311580118429)
XLA Ops:
  0.6 1.8 %constant_dynamic-slice_fusion.table_ref = f32[367,96]{1,0:T(8,128)} fusion(f32[367,1536]{1,0:T(8,128)} %param.13, s32[]{:T(128)S(6)} %select_n.3), kind=kLoop, calls=%fused_computation.1 | loop fusion | bytes 281860 | tf_op jit(solution)/shard_map/dynamic_slice | solution.py:744
  2.4 153.7 %conv_section.1 = (f32[1,256]{1,0:T(1,128)}, f32[96,512]{1,0:T(8,128)}, bf16[3,288,1536]{2,1,0:T(8,128)(2,1)}, f32[3,96]{1,0:T(4,128)}) custom-call(bf16[96,512]{1,0:T(8,128)(2,1)} %seq_ref.1, bf16[3,288,1536]{2,1,0:T(8,128)(2,1)} %bitcast.13, f32[3,96]{1,0:T(4,128)} %gain_in.1, f32[96,512]{1,0:T(8,128)} %tower_hbm.1, ...), custom_call_target="tpu_custom_call" | custom-call | tf_op jit(solution)/shard_map/conv_section/pallas_call | solution.py:649
  156.1 0.0 copy-start.2
  156.1 0.0 copy-start
  156.1 0.0 copy-start.1
  156.1 4.9 %convert_bitcast_fusion = f32[3,96,3,1536]{3,1,2,0:T(8,128)} fusion(bf16[3,3,96,1536]{3,2,1,0:T(8,128)(2,1)} %bitcast.14), kind=kLoop, calls=%fused_computation | loop fusion | flops 1327104 | bytes 7962624 | tf_op jit(solution)/shard_map/convert_element_type | solution.py:757
  161.0 0.0 copy-done.2
  161.0 0.6 copy.17
  161.6 0.0 copy-done
  161.6 0.7 copy.18
  162.3 0.0 copy-done.1
  162.3 0.6 copy.19
Async XLA Ops:
  156.1 4.9 %copy-start.2 = (f32[1,256]{1,0:T(1,128)S(1)}, f32[1,256]{1,0:T(1,128)}, u32[]{:S(2)}) copy-start(f32[1,256]{1,0:T(1,128)} %get-tuple-element.8) | copy-start | bytes 3076
  156.1 5.5 %copy-start = (f32[96,512]{1,0:T(8,128)S(1)}, f32[96,512]{1,0:T(8,128)}, u32[]{:S(2)}) copy-start(f32[96,512]{1,0:T(8,128)} %get-tuple-element.17) | copy-start | bytes 589828
  156.1 6.2 %copy-start.1 = (f32[3,96]{1,0:T(4,128)S(1)}, f32[3,96]{1,0:T(4,128)}, u32[]{:S(2)}) copy-start(f32[3,96]{1,0:T(4,128)} %get-tuple-element.19) | copy-start | bytes 3460

commit v4 on v3

--- a/solution.py
+++ b/solution.py
@@ -16,6 +16,7 @@
 SIDE = 4
 SEQ = 8
 JUNC = 256
+CAP = 128
 MESH = pl.DeviceIdType.MESH
 EPSILON = 1e-06
 ROOT = math.sqrt(CHANNELS)
@@ -75,6 +76,7 @@
     wt,
     meta_all,
     pick,
+    slots,
     donor_hot,
     tissue_rows,
     state3,
@@ -215,14 +217,6 @@
 
     halo_start(seq_ref, halo_rx, 0)
 
-    meta_all[s] = owner_ref[...] * LENGTH + offset_ref[...]
-    for d in range(1, SEQ):
-        begin(
-            remote(
-                meta_all.at[s], meta_all.at[s], meta_send.at[d - 1], meta_recv.at[d - 1], {"seq": speer(d)}
-            )
-        )
-
     gain = gain_ref[...]
     high = gain.astype(BF16).astype(F32)
     rest = gain - high
@@ -266,14 +260,39 @@
         tissue_rows[...] = dot(t_high, hot) + dot(t_mid, hot) + dot(t_low, hot)
         donor_hot[...] = one_hot(LENGTH, donor_ref[...], 0)
 
-    def prepare_picks():
+    def send_meta():
+        owner = owner_ref[...]
+        member = one_hot(16, owner, 0)
+        first = lax.broadcasted_iota(jnp.int32, (JUNC, JUNC), 0)
+        second = lax.broadcasted_iota(jnp.int32, (JUNC, JUNC), 1)
+        rank = dot(member, jnp.where(first <= second, 1.0, 0.0).astype(BF16))
+        slot = jnp.sum(member.astype(F32) * rank, axis=0, keepdims=True) - 1.0
+        slot = slot.astype(jnp.int32)
+        meta_all[s] = (slot * SEQ + owner) * LENGTH + offset_ref[...]
+        for d in range(1, SEQ):
+            begin(
+                remote(
+                    meta_all.at[s], meta_all.at[s], meta_send.at[d - 1], meta_recv.at[d - 1], {"seq": speer(d)}
+                )
+            )
+        ids = lax.broadcasted_iota(jnp.int32, (CAP, JUNC), 0)
+        for d in range(SEQ):
+            mine = (ids == slot) & (owner == speer(d))
+            slots[CAP * d : CAP * d + CAP, :] = jnp.where(mine, 1.0, 0.0).astype(BF16)
+
+    def wait_meta():
         for d in range(1, SEQ):
             src = speer(SEQ - d)
             remote(
                 meta_all.at[src], meta_all.at[src], meta_send.at[d - 1], meta_recv.at[d - 1], {"seq": src}
             ).wait_recv()
-        for d in range(SEQ):
-            pick[d] = one_hot(LENGTH, meta_all[speer(d)], s * LENGTH)
+
+    def prepare_picks(which):
+        for d in which:
+            row = meta_all[speer(d)]
+            place = one_hot(LENGTH, row & (SEQ * LENGTH - 1), s * LENGTH)
+            slot = one_hot(CAP, lax.shift_right_logical(row, 12), 0)
+            pick[:, CAP * d : CAP * d + CAP] = dot_rows(place, slot).astype(BF16)
 
     for layer in range(LAYERS):
         reach = 2 ** (layer + 3)
@@ -320,6 +339,7 @@
             go(me, 1, xpeer(d))
 
         if layer == 0:
+            send_meta()
             prepare_tissues()
             load_w.wait()
         if layer > 0:
@@ -367,23 +387,28 @@
 
         for d in (0,) + NEAR:
             group = lax.rem(mx + d, SIDE)
-            if d == 0:
-                for e in NEAR:
-                    arrived(ypeer(e), 0)
-            else:
+            if d > 0:
                 arrived(xpeer(d), 1)
-                for e in NEAR:
-                    block = group * SIDE + lax.rem(my + e, SIDE)
-                    arrived(block, 0)
+            hide(group * SIDE + my, 0)
+
+            def next_block(e, carry, d=d, group=group, arrived=arrived, hide=hide):
+                block = group * SIDE + lax.rem(my + e, SIDE)
+                arrived(block, 0)
+                if d > 0:
                     arrived(block, 1)
-            lax.fori_loop(group * SIDE, group * SIDE + SIDE, hide, 0)
+                return hide(block, carry)
+
+            lax.fori_loop(1, SIDE, next_block, 0)
             span = pl.ds(pl.multiple_of(group * 384, 128), 384)
             part = dot(w_ref[layer, :, span], hid[layer, span, :])
             if d == 0:
                 ysum[...] = part
                 transpose_weights(layer)
                 if layer == 1:
-                    prepare_picks()
+                    wait_meta()
+                    prepare_picks(range(0, 4))
+                if layer == 2:
+                    prepare_picks(range(4, 8))
             elif d != NEAR[-1]:
                 ysum[...] += part
             else:
@@ -399,49 +424,53 @@
         else:
             state3[...] = state[:, 0:LENGTH].astype(BF16)
 
+    def acc_copy(d):
+        return remote(
+            acc_tx.at[:, CAP * d : CAP * d + CAP],
+            acc_rx.at[:, CAP * (SEQ - d) : CAP * (SEQ - d) + CAP],
+            acc_send.at[d - 1],
+            acc_recv.at[d - 1],
+            {"seq": speer(d)},
+        )
+
+    def ab_copy(d):
+        return remote(
+            ab_tx.at[:, CAP * d : CAP * d + CAP],
+            ab_rx.at[:, CAP * (SEQ - d) : CAP * (SEQ - d) + CAP],
+            ab_send.at[d - 1],
+            ab_recv.at[d - 1],
+            {"seq": speer(d)},
+        )
+
+    acc_tx[...] = dot(state3[...], pick[...]).astype(BF16)
     for d in range(1, SEQ):
-        acc_tx[d - 1] = dot(state3[...], pick[d]).astype(BF16)
-        begin(
-            remote(
-                acc_tx.at[d - 1], acc_rx.at[d - 1], acc_send.at[d - 1], acc_recv.at[d - 1], {"seq": speer(d)}
-            )
-        )
-    vv[LAYERS - 1] = dot(w_ref[LAYERS - 1], mm[LAYERS - 1])
+        begin(acc_copy(d))
+    acc_rx[:, 0:CAP] = acc_tx[:, 0:CAP]
+    donor = dot(state3[...], donor_hot[...])
     load_tower.wait()
-    accept = dot(state3[...], pick[0])
-    donor = dot(state3[...], donor_hot[...])
-    for d in range(1, SEQ):
-        remote(
-            acc_tx.at[d - 1], acc_rx.at[d - 1], acc_send.at[d - 1], acc_recv.at[d - 1], {"seq": speer(d)}
-        ).wait_recv()
-        accept = accept + acc_rx[d - 1].astype(F32)
     weight_j = sgrad_ref[...] / ROOT
     rows_q = tissue_rows[...]
     accept_back = (weight_j * donor * rows_q).astype(BF16)
-    ab_tx[...] = accept_back
+    ab_tx[...] = dot_rows(accept_back, slots[...]).astype(BF16)
     for d in range(1, SEQ):
-        begin(
-            remote(ab_tx, ab_rx.at[d - 1], ab_send.at[d - 1], ab_recv.at[d - 1], {"seq": speer(d)})
-        )
+        begin(ab_copy(d))
+    ab_rx[:, 0:CAP] = ab_tx[:, 0:CAP]
+    vv[LAYERS - 1] = dot(w_ref[LAYERS - 1], mm[LAYERS - 1])
+    for d in range(1, SEQ):
+        acc_copy(d).wait_recv()
+    accept = dot(acc_rx[...], slots[...])
+    donor_back = weight_j * accept * rows_q
+    d_high = donor_back.astype(BF16)
+    d_low = (donor_back - d_high.astype(F32)).astype(BF16)
+    up[...] = tower_ref[...] + dot_rows(d_high, donor_hot[...]) + dot_rows(d_low, donor_hot[...])
     sc_all[me] = jnp.sum(donor * accept * rows_q, axis=0, keepdims=True) / ROOT
+    for d in range(1, SEQ):
+        ab_copy(d).wait_recv()
+    up[...] += dot_rows(ab_rx[...], pick[...])
     for d in range(1, SIDE * SIDE):
         begin(
             remote(sc_all.at[me], sc_all.at[me], sc_send.at[d - 1], sc_recv.at[d - 1], {"tp": tpeer(d)})
         )
-    donor_back = weight_j * accept * rows_q
-    d_high = donor_back.astype(BF16)
-    d_low = (donor_back - d_high.astype(F32)).astype(BF16)
-    added = (
-        dot_rows(d_high, donor_hot[...])
-        + dot_rows(d_low, donor_hot[...])
-        + dot_rows(accept_back, pick[0])
-    )
-    up[...] = tower_ref[...] + added
-    for d in range(1, SEQ):
-        remote(
-            ab_tx, ab_rx.at[d - 1], ab_send.at[d - 1], ab_recv.at[d - 1], {"seq": speer(d)}
-        ).wait_recv()
-        up[...] += dot_rows(ab_rx[d - 1], pick[SEQ - d])
 
     def w_cores(layer):
         return remote(
@@ -671,14 +700,15 @@
             pltpu.VMEM((LAYERS, 8, WIN), F32),
             pltpu.VMEM((LAYERS, CHANNELS, 3 * LOCAL), BF16),
             pltpu.VMEM((SEQ, 1, JUNC), jnp.int32),
-            pltpu.VMEM((SEQ, LENGTH, JUNC), BF16),
+            pltpu.VMEM((LENGTH, SEQ * CAP), BF16),
+            pltpu.VMEM((SEQ * CAP, JUNC), BF16),
             pltpu.VMEM((LENGTH, JUNC), BF16),
             pltpu.VMEM((LOCAL, JUNC), F32),
             pltpu.VMEM((LOCAL, LENGTH), BF16),
-            pltpu.VMEM((SEQ - 1, LOCAL, JUNC), BF16),
-            pltpu.VMEM((SEQ - 1, LOCAL, JUNC), BF16),
-            pltpu.VMEM((LOCAL, JUNC), BF16),
-            pltpu.VMEM((SEQ - 1, LOCAL, JUNC), BF16),
+            pltpu.VMEM((LOCAL, SEQ * CAP), BF16),
+            pltpu.VMEM((LOCAL, SEQ * CAP), BF16),
+            pltpu.VMEM((LOCAL, SEQ * CAP), BF16),
+            pltpu.VMEM((LOCAL, SEQ * CAP), BF16),
             pltpu.VMEM((16, 1, JUNC), F32),
             pltpu.VMEM((LOCAL, LENGTH), F32),
             pltpu.VMEM((LAYERS, LOCAL, LENGTH), BF16),

time: 163 us -> 155 us (0.951)
  Pallas kernels: 154 us -> 145 us
    pallas_call x1, Pallas kernels: 154 us -> 145 us  [section(): pl.pallas_call(section_kernel, out_shape=(jax.ShapeDtypeStruct((1, JUNC),...]
where the time goes in v4:
time: 155 us
  Pallas kernels  145 us (94%)
  other arithmetic  4.9 us (3%)
  local copies, waits for them, and re-layouts  3.62 us (2%)
    pallas_call x1, Pallas kernels, section(): pl.pallas_call(section_kernel, out_shape=(jax.ShapeDtypeStruct((1, JUNC),...  145 us
    convert_element_type x1, other arithmetic, local(): weights.reshape(LAYERS, 3, LOCAL, CHANNELS).transpose(0, 2, 1, 3)  4.9 us

profile of v4, /device:TPU:1, one launch (start us, length us, event | category | flops | bytes accessed | tf_op | source)
XLA Modules:
  0.0 154.6 jit_solution(15691638323738329832)
XLA Ops:
  0.6 1.8 %constant_dynamic-slice_fusion.table_ref = f32[367,96]{1,0:T(8,128)} fusion(f32[367,1536]{1,0:T(8,128)} %param.13, s32[]{:T(128)S(6)} %select_n.3), kind=kLoop, calls=%fused_computation.1 | loop fusion | bytes 281860 | tf_op jit(solution)/shard_map/dynamic_slice | solution.py:774
  2.4 145.5 %conv_section.1 = (f32[1,256]{1,0:T(1,128)}, f32[96,512]{1,0:T(8,128)}, bf16[3,288,1536]{2,1,0:T(8,128)(2,1)}, f32[3,96]{1,0:T(4,128)}) custom-call(bf16[96,512]{1,0:T(8,128)(2,1)} %seq_ref.1, bf16[3,288,1536]{2,1,0:T(8,128)(2,1)} %bitcast.13, f32[3,96]{1,0:T(4,128)} %gain_in.1, f32[96,512]{1,0:T(8,128)} %tower_hbm.1, ...), custom_call_target="tpu_custom_call" | custom-call | tf_op jit(solution)/shard_map/conv_section/pallas_call | solution.py:678
  147.9 0.0 copy-start.2
  147.9 0.0 copy-start
  147.9 0.0 copy-start.1
  147.9 4.9 %convert_bitcast_fusion = f32[3,96,3,1536]{3,1,2,0:T(8,128)} fusion(bf16[3,3,96,1536]{3,2,1,0:T(8,128)(2,1)} %bitcast.14), kind=kLoop, calls=%fused_computation | loop fusion | flops 1327104 | bytes 7962624 | tf_op jit(solution)/shard_map/convert_element_type | solution.py:787
  152.8 0.0 copy-done.2
  152.8 0.6 copy.17
  153.4 0.0 copy-done
  153.4 0.7 copy.18
  154.1 0.0 copy-done.1
  154.1 0.6 copy.19
Async XLA Ops:
  147.9 4.9 %copy-start.2 = (f32[1,256]{1,0:T(1,128)S(1)}, f32[1,256]{1,0:T(1,128)}, u32[]{:S(2)}) copy-start(f32[1,256]{1,0:T(1,128)} %get-tuple-element.8) | copy-start | bytes 3076
  147.9 5.5 %copy-start = (f32[96,512]{1,0:T(8,128)S(1)}, f32[96,512]{1,0:T(8,128)}, u32[]{:S(2)}) copy-start(f32[96,512]{1,0:T(8,128)} %get-tuple-element.17) | copy-start | bytes 589828
  147.9 6.2 %copy-start.1 = (f32[3,96]{1,0:T(4,128)S(1)}, f32[3,96]{1,0:T(4,128)}, u32[]{:S(2)}) copy-start(f32[3,96]{1,0:T(4,128)} %get-tuple-element.19) | copy-start | bytes 3460

commit v5 on v4

--- a/solution.py
+++ b/solution.py
@@ -51,7 +51,7 @@
     w_hbm,
     gain_in,
     tower_hbm,
-    table_ref,
+    table_hbm,
     owner_ref,
     offset_ref,
     donor_ref,
@@ -64,6 +64,7 @@
     w_ref,
     tower_ref,
     gain_ref,
+    window,
     turn,
     tab,
     gst,
@@ -100,6 +101,7 @@
     wz_tx,
     wz_rx,
     wres,
+    stage,
     gg,
     gg_all,
     halo_send,
@@ -152,7 +154,13 @@
 
     load_w = pltpu.make_async_copy(w_hbm, w_ref, load_sem.at[0])
     load_tower = pltpu.make_async_copy(tower_hbm, tower_ref, load_sem.at[1])
+    start = jnp.minimum(me * LOCAL // 128, CHANNELS // 128 - 2) * 128
+    skip = me * LOCAL - start
+    load_table = pltpu.make_async_copy(
+        table_hbm.at[:, pl.ds(pl.multiple_of(start, 128), 256)], window, load_sem.at[2]
+    )
     load_w.start()
+    load_table.start()
     load_tower.start()
 
     barrier = pltpu.get_barrier_semaphore()
@@ -249,8 +257,9 @@
         return jnp.where(ids == row_ids, 1.0, 0.0).astype(BF16)
 
     def prepare_tissues():
+        load_table.wait()
         tab[...] = jnp.zeros((384, 128), F32)
-        tab[0 : table_ref.shape[0], 0:LOCAL] = table_ref[...]
+        tab[0 : window.shape[0], :] = pltpu.roll(window[...], lax.rem(256 - skip, 256), 1)[:, 0:128]
         table = tab[...].T[0:LOCAL]
         t_high = table.astype(BF16)
         t_rest = table - t_high.astype(F32)
@@ -331,27 +340,49 @@
                     {"tp": tpeer(d)},
                 )
             )
-        for d in NEAR:
-            go(me, 0, xpeer(d))
-            go(me, 1, ypeer(d))
-        for d in NEAR:
-            go(me, 0, ypeer(d))
-            go(me, 1, xpeer(d))
-
+        def at(h, p, q):
+            dx, dy = (p, q) if h == 0 else (q, p)
+            return lax.rem(mx + dx, SIDE) * SIDE + lax.rem(my + dy, SIDE)
+
+        waited = set()
+
+        def wait_block(h, p, q, at=at, waited=waited, arrived=arrived):
+            if (h, p, q) not in waited:
+                waited.add((h, p, q))
+                arrived(at(h, p, q), h)
+
+        def relay(h, p, q, targets, at=at, go=go, wait_block=wait_block):
+            if (p, q) != (0, 0):
+                wait_block(h, p, q)
+            for target in targets:
+                go(at(h, p, q), h, at(h, *target))
+
+        def second_axis(p, relay=relay):
+            for h in range(2):
+                if p % 2 == 0:
+                    relay(h, p, 3, ((0, 1),))
+                else:
+                    relay(h, p, 1, ((0, 3),))
+
+        ahead = (3, 1)
+        for h in range(2):
+            relay(h, 0, 0, ((1, 0), (3, 0)))
+        for h in range(2):
+            relay(h, 0, 0, ((0, 1), (0, 3)))
+        for h in range(2):
+            relay(h, ahead[h], 0, ((SIDE - ahead[h], 0), (0, 1), (0, 3)))
+        for h in range(2):
+            relay(h, SIDE - ahead[h], 0, ((0, 1), (0, 3)))
+        second_axis(0)
         if layer == 0:
             send_meta()
-            prepare_tissues()
             load_w.wait()
-        if layer > 0:
+        else:
             vv[layer - 1] = dot(w_ref[layer - 1], mm[layer - 1])
-
-        for d in NEAR:
-            arrived(xpeer(d), 0)
-            for e in NEAR:
-                go(xpeer(d), 0, ypeer(e))
-            arrived(ypeer(d), 1)
-            for e in NEAR:
-                go(ypeer(d), 1, xpeer(e))
+        for h in range(2):
+            relay(h, 2, 0, ((0, 1), (0, 3)))
+        second_axis(1)
+        second_axis(3)
 
         for d in range(1, SIDE * SIDE):
             src = pw.at[layer, tpeer(SIDE * SIDE - d)]
@@ -387,23 +418,22 @@
 
         for d in (0,) + NEAR:
             group = lax.rem(mx + d, SIDE)
-            if d > 0:
-                arrived(xpeer(d), 1)
-            hide(group * SIDE + my, 0)
-
-            def next_block(e, carry, d=d, group=group, arrived=arrived, hide=hide):
-                block = group * SIDE + lax.rem(my + e, SIDE)
-                arrived(block, 0)
-                if d > 0:
-                    arrived(block, 1)
-                return hide(block, carry)
-
-            lax.fori_loop(1, SIDE, next_block, 0)
+            for e in (0,) + NEAR:
+                if d + e > 0:
+                    wait_block(0, d, e)
+                    wait_block(1, e, d)
+                if d == NEAR[-1]:
+                    hide(group * SIDE + lax.rem(my + e, SIDE), 0)
+            if d != NEAR[-1]:
+                lax.fori_loop(group * SIDE, group * SIDE + SIDE, hide, 0)
             span = pl.ds(pl.multiple_of(group * 384, 128), 384)
             part = dot(w_ref[layer, :, span], hid[layer, span, :])
             if d == 0:
                 ysum[...] = part
+                second_axis(2)
                 transpose_weights(layer)
+                if layer == 0:
+                    prepare_tissues()
                 if layer == 1:
                     wait_meta()
                     prepare_picks(range(0, 4))
@@ -525,6 +555,9 @@
             ).wait_recv()
             begin(w_share(layer, d))
 
+    def store_w(layer):
+        return pltpu.make_async_copy(stage.at[layer], wgrad_ref.at[layer], load_sem.at[3 + layer])
+
     def w_step5(layer):
         for d in range(SIDE):
             part = wres.at[layer, 1 - core, lax.rem(mz + SIDE - d, SIDE)]
@@ -533,7 +566,8 @@
             ).wait_recv()
         for h in range(2):
             for q in range(SIDE):
-                wgrad_ref[layer, 144 * h : 144 * h + 144, 384 * q : 384 * q + 384] = wres[layer, h, q]
+                stage[layer, 144 * h : 144 * h + 144, 384 * q : 384 * q + 384] = wres[layer, h, q].astype(F32)
+        store_w(layer).start()
 
     gg[...] = jnp.zeros((128, 128), F32)
     for layer in reversed(range(LAYERS)):
@@ -613,6 +647,8 @@
                 w_step3(layer)
         if layer > 0:
             w_step3(layer)
+        if layer < LAYERS - 1:
+            w_step5(layer + 1)
 
         x = (seq_ref[...] if layer == 0 else jnp.concatenate(
             [gst[layer, me, 0, :, 0:LENGTH], gst[layer, me, 1, :, 0:LENGTH]], axis=0
@@ -662,8 +698,9 @@
         src = gg_all.at[speer(SEQ - d)]
         remote(src, src, gg_send.at[d - 1], gg_recv.at[d - 1], {"seq": speer(d)}).wait_recv()
     gains_ref[...] = jnp.sum(gg_all[...], axis=0)[0:LAYERS, 0:LOCAL]
-    for layer in reversed(range(LAYERS)):
-        w_step5(layer)
+    w_step5(0)
+    for layer in range(LAYERS):
+        store_w(layer).wait()
     for copy in pending:
         copy.wait_send()
 
@@ -680,15 +717,16 @@
         out_shape=(
             jax.ShapeDtypeStruct((1, JUNC), F32),
             jax.ShapeDtypeStruct((LOCAL, LENGTH), F32),
-            jax.ShapeDtypeStruct((LAYERS, 3 * LOCAL, CHANNELS), BF16),
+            jax.ShapeDtypeStruct((LAYERS, 3 * LOCAL, CHANNELS), F32),
             jax.ShapeDtypeStruct((LAYERS, LOCAL), F32),
         ),
-        in_specs=[vmem, hbm, vmem, hbm] + [vmem] * 6,
-        out_specs=(vmem,) * 4,
+        in_specs=[vmem, hbm, vmem, hbm, hbm] + [vmem] * 5,
+        out_specs=(vmem, vmem, hbm, vmem),
         scratch_shapes=[
             pltpu.VMEM((LAYERS, 3 * LOCAL, CHANNELS), BF16),
             pltpu.VMEM((LOCAL, LENGTH), F32),
             pltpu.VMEM((LOCAL, 128), F32),
+            pltpu.VMEM((367, 256), F32),
             pltpu.VMEM((128, 128), F32),
             pltpu.VMEM((384, 128), F32),
             pltpu.VMEM((LAYERS, 16, 2, HALF, WIN), BF16),
@@ -725,6 +763,7 @@
             pltpu.VMEM((LAYERS, SIDE, 144, 384), BF16),
             pltpu.VMEM((LAYERS, 3, 144, 384), BF16),
             pltpu.VMEM((LAYERS, 2, SIDE, 144, 384), BF16),
+            pltpu.VMEM((LAYERS, 3 * LOCAL, CHANNELS), F32),
             pltpu.VMEM((128, 128), F32),
             pltpu.VMEM((SEQ, 8, 128), F32),
             dma(4, 2),
@@ -749,7 +788,7 @@
             dma(7),
             dma(LAYERS, 15),
             dma(LAYERS, 15),
-            dma(2),
+            dma(6),
         ],
         compiler_params=pltpu.CompilerParams(
             collective_id=0, has_side_effects=True, vmem_limit_bytes=62 * 1024 * 1024
@@ -771,20 +810,19 @@
     score_grad,
 ):
     stacked = conv_weight.transpose(0, 2, 1, 3).reshape(LAYERS, 3 * LOCAL, CHANNELS)
-    table = lax.dynamic_slice_in_dim(tissue_scale, lax.axis_index("tp") * LOCAL, LOCAL, 1)
     scores, grad, weights, gains = section(
         sequence_in,
         stacked,
         norm_gain,
         tower_grad,
-        table,
+        tissue_scale,
         acceptor_owner.T,
         acceptor_offset[None, :],
         donor_offset[None, :],
         tissue[None, :],
         score_grad[None, :],
     )
-    weights = weights.reshape(LAYERS, 3, LOCAL, CHANNELS).transpose(0, 2, 1, 3).astype(F32)
+    weights = weights.reshape(LAYERS, 3, LOCAL, CHANNELS).transpose(0, 2, 1, 3)
     return (scores[0], grad, weights, gains)
 
 

time: 155 us -> 153 us (0.987)
  local copies, waits for them, and re-layouts: 3.62 us -> 8.67 us
  other arithmetic: 4.9 us -> 0 us
    unnamed x9 -> x6, local copies, waits for them, and re-layouts: 1.83 us -> 8.67 us
    convert_element_type x1 -> x0, other arithmetic: 4.9 us -> none  [local(): weights.reshape(LAYERS, 3, LOCAL, CHANNELS).transpose(0, 2, 1, 3)]
    dynamic_slice x1 -> x0, local copies, waits for them, and re-layouts: 1.79 us -> none  [local(): lax.dynamic_slice_in_dim(tissue_scale, lax.axis_index('tp') * LOCAL, LOCA...]
    pallas_call x1, Pallas kernels: 145 us -> 144 us  [section(): pl.pallas_call(section_kernel, out_shape=(jax.ShapeDtypeStruct((1, JUNC),...]
where the time goes in v5:
time: 153 us
  Pallas kernels  144 us (94%)
  local copies, waits for them, and re-layouts  8.67 us (6%)
    pallas_call x1, Pallas kernels, section(): pl.pallas_call(section_kernel, out_shape=(jax.ShapeDtypeStruct((1, JUNC),...  144 us
    unnamed x6, local copies, waits for them, and re-layouts  8.67 us

profile of v5, /device:TPU:1, one launch (start us, length us, event | category | flops | bytes accessed | tf_op | source)
XLA Modules:
  0.0 153.2 jit_solution(4096186759043706034)
XLA Ops:
  0.6 143.9 %conv_section.1 = (f32[1,256]{1,0:T(1,128)}, f32[96,512]{1,0:T(8,128)}, f32[3,288,1536]{2,1,0:T(8,128)}, f32[3,96]{1,0:T(4,128)}) custom-call(bf16[96,512]{1,0:T(8,128)(2,1)} %seq_ref.1, bf16[3,288,1536]{2,1,0:T(8,128)(2,1)} %bitcast.13, f32[3,96]{1,0:T(4,128)} %gain_in.1, f32[96,512]{1,0:T(8,128)} %tower_hbm.1, f32[367,1536]{1,0:T(8,128)} %table_hbm.1, ...), custom_call_target="tpu_custom_call" | custom-call | tf_op jit(solution)/shard_map/conv_section/pallas_call | solution.py:715
  144.5 1.2 copy.18
  145.7 1.6 %copy.19 = f32[96,512]{1,0:T(8,128)} copy(f32[96,512]{1,0:T(8,128)} %get-tuple-element.17) | data formatting | bytes 393216
  147.4 0.0 copy-start
  147.4 5.2 %copy.20 = f32[3,96,3,1536]{3,1,2,0:T(8,128)} copy(f32[3,96,3,1536]{3,1,2,0:T(8,128)} %bitcast.12) | data formatting | bytes 10616832
  152.6 0.0 copy-done
  152.6 0.6 copy.21
Async XLA Ops:
  147.4 5.3 %copy-start = (f32[3,96]{1,0:T(4,128)S(1)}, f32[3,96]{1,0:T(4,128)}, u32[]{:S(2)}) copy-start(f32[3,96]{1,0:T(4,128)} %get-tuple-element.19) | copy-start | bytes 3460

commit v6 on v5

--- a/solution.py
+++ b/solution.py
@@ -101,7 +101,6 @@
     wz_tx,
     wz_rx,
     wres,
-    stage,
     gg,
     gg_all,
     halo_send,
@@ -556,7 +555,7 @@
             begin(w_share(layer, d))
 
     def store_w(layer):
-        return pltpu.make_async_copy(stage.at[layer], wgrad_ref.at[layer], load_sem.at[3 + layer])
+        return pltpu.make_async_copy(wres.at[layer], wgrad_ref.at[layer], load_sem.at[3 + layer])
 
     def w_step5(layer):
         for d in range(SIDE):
@@ -564,9 +563,6 @@
             remote(
                 part, part, w_send.at[layer, 7 + d], w_recv.at[layer, 7 + d], {"seq": partner}
             ).wait_recv()
-        for h in range(2):
-            for q in range(SIDE):
-                stage[layer, 144 * h : 144 * h + 144, 384 * q : 384 * q + 384] = wres[layer, h, q].astype(F32)
         store_w(layer).start()
 
     gg[...] = jnp.zeros((128, 128), F32)
@@ -582,16 +578,50 @@
             return jnp.concatenate(rolled, axis=0)
 
         inner_g = shifted(jnp.concatenate([g, jnp.zeros((LOCAL, 128), F32)], axis=1)).astype(BF16)
+
+        def chunk(h, index, window, layer=layer):
+            rows = pl.ds(pl.multiple_of(768 * h + 192 * index, 16), 192)
+            return dot(wt[layer, rows, :], window)
+
+        def rs_one(h, c, d, layer=layer):
+            return remote(
+                pab.at[layer, h, c, d - 1],
+                rx.at[layer, h, c, d - 1],
+                rs_send.at[layer, h, c, d - 1],
+                rs_recv.at[layer, h, c, d - 1],
+                {"tp": xpeer(d) if h == 0 else ypeer(d)},
+            )
+
+        def rs_two(h, c, d, layer=layer):
+            index = lax.rem((my if h == 0 else mx) + d, SIDE)
+            return remote(
+                sab.at[layer, h, c, index],
+                ry.at[layer, h, c, d - 1],
+                rs_send.at[layer, h, c, 2 + d],
+                rs_recv.at[layer, h, c, 2 + d],
+                {"tp": ypeer(d) if h == 0 else xpeer(d)},
+            )
+
+        def partials(c, window, layer=layer, chunk=chunk, rs_one=rs_one):
+            for d in NEAR:
+                for h in range(2):
+                    base = mx if h == 0 else my
+                    pab[layer, h, c, d - 1] = chunk(h, lax.rem(base + d, SIDE), window).astype(BF16)
+                    begin(rs_one(h, c, d))
+            for h in range(2):
+                own = chunk(h, mx if h == 0 else my, window)
+                sf[h, c] = own.reshape(SIDE, HALF, 256)
+
+        partials(0, inner_g[:, 128:384])
         for q in range(3):
             part = dot_rows(inner_g, hid[layer, 512 * q : 512 * q + 512, :]).astype(BF16)
             for h in range(2):
                 wg[layer, h, :, 512 * q : 512 * q + 512] = part[144 * h : 144 * h + 144]
         begin(w_cores(layer))
-        if layer < LAYERS - 1:
-            w_step4(layer + 1)
         halo_wait(gbuf.at[layer], halo_b.at[layer], layer + 1)
         full_g = shifted(jnp.concatenate([g, halo_tile(halo_b.at[layer])], axis=1))
         full_g = full_g[:, 0:LENGTH]
+        partials(1, jnp.concatenate([full_g[:, 0:128], full_g[:, 384:512]], axis=1).astype(BF16))
         inn[layer, me] = jnp.sum(full_g * vv[layer], axis=0, keepdims=True)
         for d in range(1, SIDE * SIDE):
             begin(
@@ -603,47 +633,18 @@
                     {"tp": tpeer(d)},
                 )
             )
-        full_g = full_g.astype(BF16)
-
-        def chunk(h, index, full_g=full_g, layer=layer):
-            rows = pl.ds(pl.multiple_of(768 * h + 192 * index, 16), 192)
-            return dot(wt[layer, rows, :], full_g)
-
-        def rs_one(h, d, layer=layer):
-            return remote(
-                pab.at[layer, h, d - 1],
-                rx.at[layer, h, d - 1],
-                rs_send.at[layer, h, d - 1],
-                rs_recv.at[layer, h, d - 1],
-                {"tp": xpeer(d) if h == 0 else ypeer(d)},
-            )
-
-        def rs_two(h, d, layer=layer):
-            index = lax.rem((my if h == 0 else mx) + d, SIDE)
-            return remote(
-                sab.at[layer, h, index],
-                ry.at[layer, h, d - 1],
-                rs_send.at[layer, h, 2 + d],
-                rs_recv.at[layer, h, 2 + d],
-                {"tp": ypeer(d) if h == 0 else xpeer(d)},
-            )
-
-        for d in NEAR:
+        if layer < LAYERS - 1:
+            w_step4(layer + 1)
+        w_step2(layer)
+        for c in range(2):
             for h in range(2):
-                base = mx if h == 0 else my
-                pab[layer, h, d - 1] = chunk(h, lax.rem(base + d, SIDE)).astype(BF16)
-                begin(rs_one(h, d))
-        for h in range(2):
-            sf[h] = chunk(h, mx if h == 0 else my).reshape(SIDE, HALF, LENGTH)
-        w_step2(layer)
-        for h in range(2):
-            for d in NEAR:
-                rs_one(h, d).wait_recv()
-                sf[h] += rx[layer, h, d - 1].astype(F32).reshape(SIDE, HALF, LENGTH)
-            sab[layer, h] = sf[h].astype(BF16)
-            for d in NEAR:
-                begin(rs_two(h, d))
-            if h == 0 and layer == 0:
+                for d in NEAR:
+                    rs_one(h, c, d).wait_recv()
+                    sf[h, c] += rx[layer, h, c, d - 1].astype(F32).reshape(SIDE, HALF, 256)
+                sab[layer, h, c] = sf[h, c].astype(BF16)
+                for d in NEAR:
+                    begin(rs_two(h, c, d))
+            if c == 0 and layer == 0:
                 w_step3(layer)
         if layer > 0:
             w_step3(layer)
@@ -663,11 +664,15 @@
         )
         halves = []
         for h in range(2):
-            back = sf[h, my if h == 0 else mx]
-            for d in NEAR:
-                rs_two(h, d).wait_recv()
-                back = back + ry[layer, h, d - 1].astype(F32)
-            halves.append(back)
+            sides = []
+            for c in range(2):
+                back = sf[h, c, my if h == 0 else mx]
+                for d in NEAR:
+                    rs_two(h, c, d).wait_recv()
+                    back = back + ry[layer, h, c, d - 1].astype(F32)
+                sides.append(back)
+            middle, edges = sides
+            halves.append(jnp.concatenate([edges[:, 0:128], middle, edges[:, 128:256]], axis=1))
         back_pre = jnp.concatenate(halves, axis=0) * slope
         back_norm = back_pre * g_col
         gain_col = jnp.sum(back_pre * norm, axis=1, keepdims=True)
@@ -717,7 +722,7 @@
         out_shape=(
             jax.ShapeDtypeStruct((1, JUNC), F32),
             jax.ShapeDtypeStruct((LOCAL, LENGTH), F32),
-            jax.ShapeDtypeStruct((LAYERS, 3 * LOCAL, CHANNELS), F32),
+            jax.ShapeDtypeStruct((LAYERS, 2, SIDE, 144, 384), BF16),
             jax.ShapeDtypeStruct((LAYERS, LOCAL), F32),
         ),
         in_specs=[vmem, hbm, vmem, hbm, hbm] + [vmem] * 5,
@@ -752,18 +757,17 @@
             pltpu.VMEM((LAYERS, LOCAL, LENGTH), BF16),
             pltpu.VMEM((2, LOCAL, 128), BF16),
             pltpu.VMEM((LAYERS, 2, LOCAL, 128), BF16),
-            pltpu.VMEM((LAYERS, 2, 3, 192, LENGTH), BF16),
-            pltpu.VMEM((LAYERS, 2, 3, 192, LENGTH), BF16),
-            pltpu.VMEM((2, SIDE, HALF, LENGTH), F32),
-            pltpu.VMEM((LAYERS, 2, SIDE, HALF, LENGTH), BF16),
-            pltpu.VMEM((LAYERS, 2, 3, HALF, LENGTH), BF16),
+            pltpu.VMEM((LAYERS, 2, 2, 3, 192, 256), BF16),
+            pltpu.VMEM((LAYERS, 2, 2, 3, 192, 256), BF16),
+            pltpu.VMEM((2, 2, SIDE, HALF, 256), F32),
+            pltpu.VMEM((LAYERS, 2, 2, SIDE, HALF, 256), BF16),
+            pltpu.VMEM((LAYERS, 2, 2, 3, HALF, 256), BF16),
             pltpu.VMEM((LAYERS, 16, 1, LENGTH), F32),
             pltpu.VMEM((LAYERS, 2, 144, CHANNELS), BF16),
             pltpu.VMEM((LAYERS, 144, CHANNELS), BF16),
             pltpu.VMEM((LAYERS, SIDE, 144, 384), BF16),
             pltpu.VMEM((LAYERS, 3, 144, 384), BF16),
             pltpu.VMEM((LAYERS, 2, SIDE, 144, 384), BF16),
-            pltpu.VMEM((LAYERS, 3 * LOCAL, CHANNELS), F32),
             pltpu.VMEM((128, 128), F32),
             pltpu.VMEM((SEQ, 8, 128), F32),
             dma(4, 2),
@@ -778,8 +782,8 @@
             dma(7),
             dma(15),
             dma(15),
-            dma(LAYERS, 2, 6),
-            dma(LAYERS, 2, 6),
+            dma(LAYERS, 2, 2, 6),
+            dma(LAYERS, 2, 2, 6),
             dma(LAYERS, 15),
             dma(LAYERS, 15),
             dma(LAYERS, 11),
@@ -795,6 +799,43 @@
         ),
         name="conv_section",
     )(*operands)
+
+
+def finish_kernel(w_ref, scores_ref, grad_ref, gains_ref, w_out, scores_out, grad_out, gains_out):
+    for q in range(SIDE):
+        w_out[0, :, 384 * q : 384 * q + 384] = w_ref[0, 0, q].astype(F32)
+    scores_out[...] = scores_ref[...]
+    grad_out[...] = grad_ref[...]
+    gains_out[...] = gains_ref[...]
+
+
+def finish(weights, scores, grad, gains):
+    def whole(x):
+        return pl.BlockSpec(x.shape, lambda i, j: (0, 0))
+
+    return pl.pallas_call(
+        finish_kernel,
+        grid=(LAYERS, 2),
+        out_shape=(
+            jax.ShapeDtypeStruct((LAYERS, 3 * LOCAL, CHANNELS), F32),
+            jax.ShapeDtypeStruct(scores.shape, F32),
+            jax.ShapeDtypeStruct(grad.shape, F32),
+            jax.ShapeDtypeStruct(gains.shape, F32),
+        ),
+        in_specs=[
+            pl.BlockSpec((1, 1, SIDE, 144, 384), lambda i, j: (i, j, 0, 0, 0)),
+            whole(scores),
+            whole(grad),
+            whole(gains),
+        ],
+        out_specs=(
+            pl.BlockSpec((1, 144, CHANNELS), lambda i, j: (i, j, 0)),
+            whole(scores),
+            whole(grad),
+            whole(gains),
+        ),
+        name="finish",
+    )(weights, scores, grad, gains)
 
 
 def local(
@@ -822,6 +863,7 @@
         tissue[None, :],
         score_grad[None, :],
     )
+    weights, scores, grad, gains = finish(weights, scores, grad, gains)
     weights = weights.reshape(LAYERS, 3, LOCAL, CHANNELS).transpose(0, 2, 1, 3)
     return (scores[0], grad, weights, gains)
 

time: 153 us -> 142 us (0.928)
  local copies, waits for them, and re-layouts: 8.67 us -> 0 us
  Pallas kernels: 144 us -> 141 us
    unnamed x6 -> x0, local copies, waits for them, and re-layouts: 8.67 us -> none
    pallas_call x1, Pallas kernels: 144 us -> 135 us  [section(): pl.pallas_call(section_kernel, out_shape=(jax.ShapeDtypeStruct((1, JUNC),...]
    pallas_call x0 -> x1, Pallas kernels: none -> 5.61 us  [finish(): pl.pallas_call(finish_kernel, grid=(LAYERS, 2), out_shape=(jax.ShapeDtype...]
where the time goes in v6:
time: 142 us
  Pallas kernels  141 us (99%)
    pallas_call x1, Pallas kernels, section(): pl.pallas_call(section_kernel, out_shape=(jax.ShapeDtypeStruct((1, JUNC),...  135 us
    pallas_call x1, Pallas kernels, finish(): pl.pallas_call(finish_kernel, grid=(LAYERS, 2), out_shape=(jax.ShapeDtype...  5.61 us

profile of v6, /device:TPU:1, one launch (start us, length us, event | category | flops | bytes accessed | tf_op | source)
XLA Modules:
  0.0 141.7 jit_solution(16973775214206914029)
XLA Ops:
  0.6 135.4 %conv_section.1 = (f32[1,256]{1,0:T(1,128)}, f32[96,512]{1,0:T(8,128)}, bf16[3,2,4,144,384]{4,3,2,1,0:T(8,128)(2,1)}, f32[3,96]{1,0:T(4,128)}) custom-call(bf16[96,512]{1,0:T(8,128)(2,1)} %seq_ref.1, bf16[3,288,1536]{2,1,0:T(8,128)(2,1)} %bitcast.12, f32[3,96]{1,0:T(4,128)} %gain_in.1, f32[96,512]{1,0:T(8,128)} %tower_hbm.1, f32[367,1536]{1,0:T(8,128)} %table_hbm.1, ...), custom_call_target="tpu_custom_call" | custom-call | tf_op jit(solution)/shard_map/conv_section/pallas_call | solution.py:720
  136.1 5.6 %finish.1 = (f32[3,288,1536]{2,1,0:T(8,128)}, f32[1,256]{1,0:T(1,128)}, f32[96,512]{1,0:T(8,128)}, f32[3,96]{1,0:T(4,128)}) custom-call(bf16[3,2,4,144,384]{4,3,2,1,0:T(8,128)(2,1)} %get-tuple-element.12.w_ref, f32[1,256]{1,0:T(1,128)} %get-tuple-element.13.scores_ref, f32[96,512]{1,0:T(8,128)} %get-tuple-element.14.grad_ref, ...), custom_call_target="tpu_custom_call" | custom-call | tf_op jit(solution)/shard_map/finish/pallas_call | solution.py:816

commit v7 on v6

--- a/solution.py
+++ b/solution.py
@@ -125,6 +125,8 @@
     gg_recv,
     pw_send,
     pw_recv,
+    tile_send,
+    tile_recv,
     load_sem,
 ):
     s = lax.axis_index("seq")
@@ -234,10 +236,15 @@
 
     for h in range(2):
         gst[0, me, h, :, 0:512] = seq_ref[HALF * h : HALF * h + HALF, :]
-    halo_wait(seq_ref, halo_rx, 0)
-    tile = jnp.where(in_gain, packed, halo_tile(halo_rx)).astype(BF16)
-    for h in range(2):
-        gst[0, me, h, :, 512:640] = tile[HALF * h : HALF * h + HALF, :]
+
+    def finish_tile():
+        halo_wait(seq_ref, halo_rx, 0)
+        tile = jnp.where(in_gain, packed, halo_tile(halo_rx)).astype(BF16)
+        for h in range(2):
+            gst[0, me, h, :, 512:640] = tile[HALF * h : HALF * h + HALF, :]
+        for d in range(1, SIDE * SIDE):
+            own = gst.at[0, me, :, :, 512:640]
+            begin(remote(own, own, tile_send.at[d - 1], tile_recv.at[d - 1], {"tp": tpeer(d)}))
 
     col = lax.broadcasted_iota(jnp.int32, (LOCAL, WIN), 1)
     outside = ((s == SEQ - 1) & (col >= 512) & (col < 576)) | ((s == 0) & (col >= 576))
@@ -306,11 +313,16 @@
         reach = 2 ** (layer + 3)
         count = [0]
 
-        def go(block, h, peer, layer=layer, count=count):
+        def piece(block, h, layer=layer):
+            if layer == 0:
+                return gst.at[layer, block, h, :, 0:LENGTH]
+            return gst.at[layer, block, h]
+
+        def go(block, h, peer, layer=layer, count=count, piece=piece):
             begin(
                 remote(
-                    gst.at[layer, block, h],
-                    gst.at[layer, block, h],
+                    piece(block, h),
+                    piece(block, h),
                     gather_send.at[layer, count[0]],
                     gather_recv.at[layer, block, h],
                     {"tp": peer},
@@ -318,27 +330,32 @@
             )
             count[0] += 1
 
-        def arrived(block, h, layer=layer):
+        def arrived(block, h, layer=layer, piece=piece):
             remote(
-                gst.at[layer, block, h],
-                gst.at[layer, block, h],
+                piece(block, h),
+                piece(block, h),
                 gather_send.at[layer, 0],
                 gather_recv.at[layer, block, h],
                 {"tp": xpeer(1)},
             ).wait_recv()
 
-        squares = jnp.concatenate([gst[layer, me, 0], gst[layer, me, 1]], axis=0).astype(F32)
-        pw[layer, me] = jnp.sum(squares * squares, axis=0, keepdims=True)
-        for d in range(1, SIDE * SIDE):
-            begin(
-                remote(
-                    pw.at[layer, me],
-                    pw.at[layer, me],
-                    pw_send.at[layer, d - 1],
-                    pw_recv.at[layer, d - 1],
-                    {"tp": tpeer(d)},
+        def send_powers(layer=layer):
+            squares = jnp.concatenate([gst[layer, me, 0], gst[layer, me, 1]], axis=0).astype(F32)
+            pw[layer, me] = jnp.sum(squares * squares, axis=0, keepdims=True)
+            for d in range(1, SIDE * SIDE):
+                begin(
+                    remote(
+                        pw.at[layer, me],
+                        pw.at[layer, me],
+                        pw_send.at[layer, d - 1],
+                        pw_recv.at[layer, d - 1],
+                        {"tp": tpeer(d)},
+                    )
                 )
-            )
+
+        if layer > 0:
+            send_powers()
+
         def at(h, p, q):
             dx, dy = (p, q) if h == 0 else (q, p)
             return lax.rem(mx + dx, SIDE) * SIDE + lax.rem(my + dy, SIDE)
@@ -363,25 +380,32 @@
                 else:
                     relay(h, p, 1, ((0, 3),))
 
-        ahead = (3, 1)
         for h in range(2):
-            relay(h, 0, 0, ((1, 0), (3, 0)))
+            relay(h, 0, 0, ((1, 0), (3, 0), (2, 0)))
         for h in range(2):
             relay(h, 0, 0, ((0, 1), (0, 3)))
+        for p in (3, 1):
+            for h in range(2):
+                relay(h, p, 0, ((0, 1), (0, 3)))
         for h in range(2):
-            relay(h, ahead[h], 0, ((SIDE - ahead[h], 0), (0, 1), (0, 3)))
-        for h in range(2):
-            relay(h, SIDE - ahead[h], 0, ((0, 1), (0, 3)))
+            relay(h, 2, 0, ((0, 1), (0, 3), (0, 2)))
+        if layer == 0:
+            finish_tile()
+            send_powers()
         second_axis(0)
         if layer == 0:
             send_meta()
             load_w.wait()
+            prepare_tissues()
         else:
             vv[layer - 1] = dot(w_ref[layer - 1], mm[layer - 1])
-        for h in range(2):
-            relay(h, 2, 0, ((0, 1), (0, 3)))
         second_axis(1)
         second_axis(3)
+        if layer == 0:
+            transpose_weights(0)
+            for d in range(1, SIDE * SIDE):
+                src = gst.at[0, tpeer(SIDE * SIDE - d), :, :, 512:640]
+                remote(src, src, tile_send.at[d - 1], tile_recv.at[d - 1], {"tp": tpeer(d)}).wait_recv()
 
         for d in range(1, SIDE * SIDE):
             src = pw.at[layer, tpeer(SIDE * SIDE - d)]
@@ -429,10 +453,8 @@
             part = dot(w_ref[layer, :, span], hid[layer, span, :])
             if d == 0:
                 ysum[...] = part
-                second_axis(2)
-                transpose_weights(layer)
-                if layer == 0:
-                    prepare_tissues()
+                if layer > 0:
+                    transpose_weights(layer)
                 if layer == 1:
                     wait_meta()
                     prepare_picks(range(0, 4))
@@ -792,6 +814,8 @@
             dma(7),
             dma(LAYERS, 15),
             dma(LAYERS, 15),
+            dma(15),
+            dma(15),
             dma(6),
         ],
         compiler_params=pltpu.CompilerParams(
@@ -801,39 +825,54 @@
     )(*operands)
 
 
-def finish_kernel(w_ref, scores_ref, grad_ref, gains_ref, w_out, scores_out, grad_out, gains_out):
-    for q in range(SIDE):
-        w_out[0, :, 384 * q : 384 * q + 384] = w_ref[0, 0, q].astype(F32)
-    scores_out[...] = scores_ref[...]
-    grad_out[...] = grad_ref[...]
-    gains_out[...] = gains_ref[...]
+def finish_kernel(
+    w_in, scores_in, grad_in, gains_in, w_out, scores_out, grad_out, gains_out, wb, wf, sb, gb, nb, sem
+):
+    small = ((scores_in, sb, scores_out), (grad_in, gb, grad_out), (gains_in, nb, gains_out))
+    loads = [pltpu.make_async_copy(w_in.at[k], wb.at[k], sem.at[k]) for k in range(LAYERS)]
+    for k, (source, buffer, _) in enumerate(small):
+        loads.append(pltpu.make_async_copy(source, buffer, sem.at[LAYERS + k]))
+    for load in loads:
+        load.start()
+    stores = []
+    for k in range(LAYERS):
+        loads[k].wait()
+        for h in range(2):
+            for q in range(SIDE):
+                wf[k, 144 * h : 144 * h + 144, 384 * q : 384 * q + 384] = wb[k, h, q].astype(F32)
+            rows = pl.ds(144 * h, 144)
+            store = pltpu.make_async_copy(wf.at[k, rows], w_out.at[k, rows], sem.at[6 + 2 * k + h])
+            store.start()
+            stores.append(store)
+    for k, (_, buffer, target) in enumerate(small):
+        loads[LAYERS + k].wait()
+        store = pltpu.make_async_copy(buffer, target, sem.at[12 + k])
+        store.start()
+        stores.append(store)
+    for store in stores:
+        store.wait()
 
 
 def finish(weights, scores, grad, gains):
-    def whole(x):
-        return pl.BlockSpec(x.shape, lambda i, j: (0, 0))
-
+    hbm = pl.BlockSpec(memory_space=pl.ANY)
     return pl.pallas_call(
         finish_kernel,
-        grid=(LAYERS, 2),
         out_shape=(
             jax.ShapeDtypeStruct((LAYERS, 3 * LOCAL, CHANNELS), F32),
             jax.ShapeDtypeStruct(scores.shape, F32),
             jax.ShapeDtypeStruct(grad.shape, F32),
             jax.ShapeDtypeStruct(gains.shape, F32),
         ),
-        in_specs=[
-            pl.BlockSpec((1, 1, SIDE, 144, 384), lambda i, j: (i, j, 0, 0, 0)),
-            whole(scores),
-            whole(grad),
-            whole(gains),
+        in_specs=[hbm] * 4,
+        out_specs=(hbm,) * 4,
+        scratch_shapes=[
+            pltpu.VMEM(weights.shape, BF16),
+            pltpu.VMEM((LAYERS, 3 * LOCAL, CHANNELS), F32),
+            pltpu.VMEM(scores.shape, F32),
+            pltpu.VMEM(grad.shape, F32),
+            pltpu.VMEM(gains.shape, F32),
+            dma(15),
         ],
-        out_specs=(
-            pl.BlockSpec((1, 144, CHANNELS), lambda i, j: (i, j, 0)),
-            whole(scores),
-            whole(grad),
-            whole(gains),
-        ),
         name="finish",
     )(weights, scores, grad, gains)
 

time: 142 us -> 143 us (level)
    pallas_call x1, Pallas kernels: 135 us -> 138 us  [section(): pl.pallas_call(section_kernel, out_shape=(jax.ShapeDtypeStruct((1, JUNC),...]
    pallas_call x1, Pallas kernels: 5.61 us -> 3.76 us  [finish(): pl.pallas_call(finish_kernel, out_shape=(jax.ShapeDtypeStruct((LAYERS, 3...]
where the time goes in v7:
time: 143 us
  Pallas kernels  142 us (99%)
    pallas_call x1, Pallas kernels, section(): pl.pallas_call(section_kernel, out_shape=(jax.ShapeDtypeStruct((1, JUNC),...  138 us
    pallas_call x1, Pallas kernels, finish(): pl.pallas_call(finish_kernel, out_shape=(jax.ShapeDtypeStruct((LAYERS, 3...  3.76 us

profile of v7, /device:TPU:1, one launch (start us, length us, event | category | flops | bytes accessed | tf_op | source)
XLA Modules:
  0.0 142.8 jit_solution(17739463596510116411)
XLA Ops:
  0.6 138.2 %conv_section.1 = (f32[1,256]{1,0:T(1,128)}, f32[96,512]{1,0:T(8,128)}, bf16[3,2,4,144,384]{4,3,2,1,0:T(8,128)(2,1)}, f32[3,96]{1,0:T(4,128)}) custom-call(bf16[96,512]{1,0:T(8,128)(2,1)} %seq_ref.1, bf16[3,288,1536]{2,1,0:T(8,128)(2,1)} %bitcast.12, f32[3,96]{1,0:T(4,128)} %gain_in.1, f32[96,512]{1,0:T(8,128)} %tower_hbm.1, f32[367,1536]{1,0:T(8,128)} %table_hbm.1, ...), custom_call_target="tpu_custom_call" | custom-call | tf_op jit(solution)/shard_map/conv_section/pallas_call | solution.py:742
  138.9 3.8 %finish.1 = (f32[3,288,1536]{2,1,0:T(8,128)}, f32[1,256]{1,0:T(1,128)}, f32[96,512]{1,0:T(8,128)}, f32[3,96]{1,0:T(4,128)}) custom-call(bf16[3,2,4,144,384]{4,3,2,1,0:T(8,128)(2,1)} %get-tuple-element.12.w_in, f32[1,256]{1,0:T(1,128)} %get-tuple-element.13.scores_in, f32[96,512]{1,0:T(8,128)} %get-tuple-element.14.grad_in, f32[3,96]{1,0:T(4,128)} %get-tuple-element.15.gains_in), custom_call_target="tpu_custom_call" | custom-call | tf_op jit(solution)/shard_map/finish/pallas_call | solution.py:858

commit v8 on v6

--- a/solution.py
+++ b/solution.py
@@ -801,39 +801,54 @@
     )(*operands)
 
 
-def finish_kernel(w_ref, scores_ref, grad_ref, gains_ref, w_out, scores_out, grad_out, gains_out):
-    for q in range(SIDE):
-        w_out[0, :, 384 * q : 384 * q + 384] = w_ref[0, 0, q].astype(F32)
-    scores_out[...] = scores_ref[...]
-    grad_out[...] = grad_ref[...]
-    gains_out[...] = gains_ref[...]
+def finish_kernel(
+    w_in, scores_in, grad_in, gains_in, w_out, scores_out, grad_out, gains_out, wb, wf, sb, gb, nb, sem
+):
+    small = ((scores_in, sb, scores_out), (grad_in, gb, grad_out), (gains_in, nb, gains_out))
+    loads = [pltpu.make_async_copy(w_in.at[k], wb.at[k], sem.at[k]) for k in range(LAYERS)]
+    for k, (source, buffer, _) in enumerate(small):
+        loads.append(pltpu.make_async_copy(source, buffer, sem.at[LAYERS + k]))
+    for load in loads:
+        load.start()
+    stores = []
+    for k in range(LAYERS):
+        loads[k].wait()
+        for h in range(2):
+            for q in range(SIDE):
+                wf[k, 144 * h : 144 * h + 144, 384 * q : 384 * q + 384] = wb[k, h, q].astype(F32)
+            rows = pl.ds(144 * h, 144)
+            store = pltpu.make_async_copy(wf.at[k, rows], w_out.at[k, rows], sem.at[6 + 2 * k + h])
+            store.start()
+            stores.append(store)
+    for k, (_, buffer, target) in enumerate(small):
+        loads[LAYERS + k].wait()
+        store = pltpu.make_async_copy(buffer, target, sem.at[12 + k])
+        store.start()
+        stores.append(store)
+    for store in stores:
+        store.wait()
 
 
 def finish(weights, scores, grad, gains):
-    def whole(x):
-        return pl.BlockSpec(x.shape, lambda i, j: (0, 0))
-
+    hbm = pl.BlockSpec(memory_space=pl.ANY)
     return pl.pallas_call(
         finish_kernel,
-        grid=(LAYERS, 2),
         out_shape=(
             jax.ShapeDtypeStruct((LAYERS, 3 * LOCAL, CHANNELS), F32),
             jax.ShapeDtypeStruct(scores.shape, F32),
             jax.ShapeDtypeStruct(grad.shape, F32),
             jax.ShapeDtypeStruct(gains.shape, F32),
         ),
-        in_specs=[
-            pl.BlockSpec((1, 1, SIDE, 144, 384), lambda i, j: (i, j, 0, 0, 0)),
-            whole(scores),
-            whole(grad),
-            whole(gains),
+        in_specs=[hbm] * 4,
+        out_specs=(hbm,) * 4,
+        scratch_shapes=[
+            pltpu.VMEM(weights.shape, BF16),
+            pltpu.VMEM((LAYERS, 3 * LOCAL, CHANNELS), F32),
+            pltpu.VMEM(scores.shape, F32),
+            pltpu.VMEM(grad.shape, F32),
+            pltpu.VMEM(gains.shape, F32),
+            dma(15),
         ],
-        out_specs=(
-            pl.BlockSpec((1, 144, CHANNELS), lambda i, j: (i, j, 0)),
-            whole(scores),
-            whole(grad),
-            whole(gains),
-        ),
         name="finish",
     )(weights, scores, grad, gains)
 

time: 142 us -> 140 us (0.986)
  Pallas kernels: 141 us -> 139 us
    pallas_call x1, Pallas kernels: 5.61 us -> 3.76 us  [finish(): pl.pallas_call(finish_kernel, out_shape=(jax.ShapeDtypeStruct((LAYERS, 3...]
where the time goes in v8:
time: 140 us
  Pallas kernels  139 us (99%)
    pallas_call x1, Pallas kernels, section(): pl.pallas_call(section_kernel, out_shape=(jax.ShapeDtypeStruct((1, JUNC),...  135 us
    pallas_call x1, Pallas kernels, finish(): pl.pallas_call(finish_kernel, out_shape=(jax.ShapeDtypeStruct((LAYERS, 3...  3.76 us

profile of v8, /device:TPU:1, one launch (start us, length us, event | category | flops | bytes accessed | tf_op | source)
XLA Modules:
  0.0 140.0 jit_solution(4835556208819991160)
XLA Ops:
  0.6 135.4 %conv_section.1 = (f32[1,256]{1,0:T(1,128)}, f32[96,512]{1,0:T(8,128)}, bf16[3,2,4,144,384]{4,3,2,1,0:T(8,128)(2,1)}, f32[3,96]{1,0:T(4,128)}) custom-call(bf16[96,512]{1,0:T(8,128)(2,1)} %seq_ref.1, bf16[3,288,1536]{2,1,0:T(8,128)(2,1)} %bitcast.12, f32[3,96]{1,0:T(4,128)} %gain_in.1, f32[96,512]{1,0:T(8,128)} %tower_hbm.1, f32[367,1536]{1,0:T(8,128)} %table_hbm.1, ...), custom_call_target="tpu_custom_call" | custom-call | tf_op jit(solution)/shard_map/conv_section/pallas_call | solution.py:720
  136.1 3.8 %finish.1 = (f32[3,288,1536]{2,1,0:T(8,128)}, f32[1,256]{1,0:T(1,128)}, f32[96,512]{1,0:T(8,128)}, f32[3,96]{1,0:T(4,128)}) custom-call(bf16[3,2,4,144,384]{4,3,2,1,0:T(8,128)(2,1)} %get-tuple-element.12.w_in, f32[1,256]{1,0:T(1,128)} %get-tuple-element.13.scores_in, f32[96,512]{1,0:T(8,128)} %get-tuple-element.14.grad_in, f32[3,96]{1,0:T(4,128)} %get-tuple-element.15.gains_in), custom_call_target="tpu_custom_call" | custom-call | tf_op jit(solution)/shard_map/finish/pallas_call | solution.py:834

commit v9 on v8

--- a/solution.py
+++ b/solution.py
@@ -603,7 +603,7 @@
             )
 
         def partials(c, window, layer=layer, chunk=chunk, rs_one=rs_one):
-            for d in NEAR:
+            for d in (2, 1, 3):
                 for h in range(2):
                     base = mx if h == 0 else my
                     pab[layer, h, c, d - 1] = chunk(h, lax.rem(base + d, SIDE), window).astype(BF16)

time: 140 us -> 140 us (level)
  no operation moved by 1% of the time
where the time goes in v9:
time: 140 us; the launch traced here: 139 us
  Pallas kernels  139 us (99%)
    pallas_call x1, Pallas kernels, section(): pl.pallas_call(section_kernel, out_shape=(jax.ShapeDtypeStruct((1, JUNC),...  135 us
    pallas_call x1, Pallas kernels, finish(): pl.pallas_call(finish_kernel, out_shape=(jax.ShapeDtypeStruct((LAYERS, 3...  3.76 us

profile of v9, /device:TPU:1, one launch (start us, length us, event | category | flops | bytes accessed | tf_op | source)
XLA Modules:
  0.0 139.4 jit_solution(4589137709784335205)
XLA Ops:
  0.6 134.8 %conv_section.1 = (f32[1,256]{1,0:T(1,128)}, f32[96,512]{1,0:T(8,128)}, bf16[3,2,4,144,384]{4,3,2,1,0:T(8,128)(2,1)}, f32[3,96]{1,0:T(4,128)}) custom-call(bf16[96,512]{1,0:T(8,128)(2,1)} %seq_ref.1, bf16[3,288,1536]{2,1,0:T(8,128)(2,1)} %bitcast.12, f32[3,96]{1,0:T(4,128)} %gain_in.1, f32[96,512]{1,0:T(8,128)} %tower_hbm.1, f32[367,1536]{1,0:T(8,128)} %table_hbm.1, ...), custom_call_target="tpu_custom_call" | custom-call | tf_op jit(solution)/shard_map/conv_section/pallas_call | solution.py:720
  135.4 3.8 %finish.1 = (f32[3,288,1536]{2,1,0:T(8,128)}, f32[1,256]{1,0:T(1,128)}, f32[96,512]{1,0:T(8,128)}, f32[3,96]{1,0:T(4,128)}) custom-call(bf16[3,2,4,144,384]{4,3,2,1,0:T(8,128)(2,1)} %get-tuple-element.12.w_in, f32[1,256]{1,0:T(1,128)} %get-tuple-element.13.scores_in, f32[96,512]{1,0:T(8,128)} %get-tuple-element.14.grad_in, f32[3,96]{1,0:T(4,128)} %get-tuple-element.15.gains_in), custom_call_target="tpu_custom_call" | custom-call | tf_op jit(solution)/shard_map/finish/pallas_call | solution.py:834
